TPU v7x, 256 devices: a whole 4x4x8 slice. The times are simulated.
256 devices in a mesh: set: 32 (over y, x, core), path: 8 (over z).
Axes of the slice: x: 4, y: 4, z: 8, core: 2. Of those that a mesh axis runs over, the one named last changes fastest.
Arguments:
- start_state: float32 [4096, 2048], P(('path', 'set')), may hold values from -6 to 6
- shocks: bfloat16 [2, 4096, 2048], P(None, ('path', 'set')), may hold values from -6 to 6
- loading: bfloat16 [2048, 2048], replicated, may hold values from -0.125 to 0.125
- decay: float32 [2048], replicated, may hold values from 0.5 to 1
- factor_lists: int32 [4096, 64], P('set'), may hold values from 0 to 2047, all different within a row
- delta: bfloat16 [4096, 64], P('set'), may hold values from -0.75 to 0.75
- gamma: bfloat16 [4096, 64, 64], P('set'), may hold values from -0.09375 to 0.09375
- currency: int32 [4096], P('set'), may hold values from 0 to 15
- owner: int32 [4096], P('set'), may hold values from 0 to 255
Outputs:
- exposure: float32 [2, 256, 4096], P(None, 'set', 'path')
- end_state: float32 [4096, 2048], P(('path', 'set'))
Inputs may be any that keep to these rules, and one draw needn't show every extreme that they name: `factor_lists`: the 64 factors of one netting set are different.
All inputs are finite; a program needn't handle non-finite values.
Results may differ from a plain program's by a relative error of at most 0.004.
Values may be sent and summed in bfloat16 or wider, within the bound.
No kernel may reach another device: no remote copies, remote signals or barrier semaphores. Data moves between devices by JAX's collectives and lax.ppermute only.
A program may use at most 64 MiB of HBM per device.

v0:
```python
import math

import jax
import jax.numpy as jnp
from jax import lax
from jax.sharding import PartitionSpec as P

NB = 16
STEPS = 2
PDEV = 16
CP_DEV = 8


def value_block(slab, lists_b, delta_b, gamma_b, cur_b):
    rows = slab.shape[0]
    count = lists_b.shape[0]
    picked = jnp.take(slab, lists_b.reshape(-1), axis=1).reshape(rows, count, lists_b.shape[1])
    curved = jnp.einsum("psk,skl->psl", picked, gamma_b, preferred_element_type=jnp.float32)
    linear = delta_b.astype(jnp.float32)[None] + 0.5 * curved
    local = jnp.sum(picked.astype(jnp.float32) * linear, axis=2)
    rates = jnp.exp(0.2 * jnp.take(slab, cur_b, axis=1).astype(jnp.float32))
    return (local * rates).T


def revalue(slab, lists, delta, gamma, cur):
    total = lists.shape[0]
    width = math.gcd(16, total)
    blocks = total // width
    depth = lists.shape[1]
    stacked = lax.map(
        lambda a: value_block(slab, a[0], a[1], a[2], a[3]),
        (
            lists.reshape(blocks, width, depth),
            delta.reshape(blocks, width, depth),
            gamma.reshape(blocks, width, depth, depth),
            cur.reshape(blocks, width),
        ),
    )
    return stacked.reshape(total, slab.shape[0])


def regress(gram, moments, total):
    size = gram.shape[0]
    chol = jnp.linalg.cholesky(gram / total + 0.001 * jnp.eye(size, dtype=jnp.float32))
    middle = lax.linalg.triangular_solve(chol, moments / total, left_side=True, lower=True)
    return lax.linalg.triangular_solve(chol, middle, left_side=True, lower=True, transpose_a=True)


def per_device(start_state, shocks, loading, decay, factor_lists, delta, gamma, currency, owner):
    high = lax.Precision.HIGHEST
    groups = lax.axis_size("set")
    member = lax.axis_index("set")
    total_paths = PDEV * groups * lax.axis_size("path")
    set_count = factor_lists.shape[0]
    onehot = (owner[None, :] == jnp.arange(CP_DEV * groups, dtype=jnp.int32)[:, None]).astype(
        jnp.float32
    )
    state = start_state
    slabs = []
    evaluated = []
    for step in range(STEPS):
        state = decay[None, :] * state + jnp.dot(
            shocks[step], loading, preferred_element_type=jnp.float32
        )
        slab = state.astype(jnp.bfloat16)
        slabs.append(slab)
        piece = lax.all_gather(slab, "set", axis=0, tiled=True)
        evaluate_values = revalue(piece, factor_lists, delta, gamma, currency)
        evaluated.append(
            jnp.concatenate([evaluate_values, piece[:, :NB].astype(jnp.float32).T], axis=0)
        )
    results = []
    for step in range(STEPS):
        values = evaluated[step][:set_count]
        factors = evaluated[step][set_count:]
        summed = lax.psum(jnp.dot(onehot, values, precision=high), "set")
        netted = lax.dynamic_slice_in_dim(summed, member * CP_DEV, CP_DEV, 0)
        ones = jnp.ones((1, values.shape[1]), jnp.float32)
        basis = jnp.concatenate([ones, factors], axis=0)
        gram, moments = lax.psum(
            (jnp.dot(basis, basis.T, precision=high), jnp.dot(basis, netted.T, precision=high)),
            "path",
        )
        coef = regress(gram, moments, total_paths)
        fitted = jnp.dot(coef.T, basis, precision=high)
        results.append(jnp.maximum(netted - 0.9 * fitted, 0.0))
    return (jnp.stack(results), state)


def solution(mesh):
    return jax.shard_map(
        per_device,
        mesh=mesh,
        in_specs=(
            P(("path", "set"), None),
            P(None, ("path", "set"), None),
            P(),
            P(),
            P("set", None),
            P("set", None),
            P("set", None, None),
            P("set"),
            P("set"),
        ),
        out_specs=(P(None, "set", "path"), P(("path", "set"), None)),
        check_vma=False,
    )
```

profile of v0, /device:TPU:2, one launch (start us, length us, event | category | flops | bytes accessed | tf_op | source)
XLA Modules:
  0.0 347.8 jit_solution(17713936069963146569)
XLA Ops:
  7.2 5.4 %fusion.65 = (bf16[16,2048]{1,0:T(8,128)(2,1)}, f32[16,2048]{1,0:T(8,128)S(1)}) fusion(bf16[2048,2048]{1,0:T(8,128)(2,1)} %param.24, bf16[2,16,2048]{2,1,0:T(8,128)(2,1)} %param.23, f32[16,2048]{1,0:T(8,128)} %param.22, f32[2048]{0:T(1024)} %param.25), kind=kOutput, calls=%fused_computation.112 | convolution fusion | flops 134316032 | bytes 8790016 | tf_op jit(solution)/shard_map/dot_general | solution.py:62
  13.1 1.9 fusion.64
  16.2 4.5 %copy.13 = bf16[128,64,64]{1,2,0:T(8,128)(2,1)} copy(bf16[128,64,64]{0,2,1:T(8,128)(2,1)S(1)} %copy-done.1) | data formatting | bytes 2097152 | tf_op args[6]
  20.7 45.7 %all-gather.5.cloned.1.call-done = bf16[512,2048]{1,0:T(8,128)(2,1)} async-done(((bf16[16,2048]{1,0:T(8,128)(2,1)}), bf16[512,2048]{1,0:T(8,128)(2,1)}) %all-gather.5.cloned.1.call-update) | async-done | bytes 2097168 | tf_op jit(solution)/shard_map/all_gather | solution.py:67
  66.4 2.9 copy.17
  69.3 52.6 %while.21 = (s32[]{:T(128)}, f32[8,16,512]{2,1,0:T(8,128)S(1)}, s32[8,16,64]{2,1,0:T(8,128)S(1)}, bf16[512,2048]{0,1:T(8,128)(2,1)S(1)}, bf16[8,16,64]{2,1,0:T(8...) while((s32[]{:T(128)}, f32[8,16,512]{2,1,0:T(8,128)S(1)}, ...), condition=%wide.region_10.16_spmd, body=%wide.region_8.15_spmd.sunk | while | flops 70291552 | bytes 6755201 | solution.py:30
  70.0 4.0 %gather_fusion.2 = bf16[1024,512]{1,0:T(8,128)(2,1)S(1)} fusion(bf16[512,2048]{0,1:T(8,128)(2,1)S(1)} %get-tuple-element.254, s32[1024]{0:T(1024)S(1)} %fusion.90), kind=kCustom, calls=%fused_computation.2.clone.clone.1 | custom fusion | bytes 2101248 | tf_op jit(solution)/shard_map/while/body/eval_jaxpr/jit(_take)/gather | solution.py:17
  76.6 4.0 %gather_fusion.2 = bf16[1024,512]{1,0:T(8,128)(2,1)S(1)} fusion(bf16[512,2048]{0,1:T(8,128)(2,1)S(1)} %get-tuple-element.254, s32[1024]{0:T(1024)S(1)} %fusion.90), kind=kCustom, calls=%fused_computation.2.clone.clone.1 | custom fusion | bytes 2101248 | tf_op jit(solution)/shard_map/while/body/eval_jaxpr/jit(_take)/gather | solution.py:17
  80.8 1.5 fusion.91
  83.2 4.0 %gather_fusion.2 = bf16[1024,512]{1,0:T(8,128)(2,1)S(1)} fusion(bf16[512,2048]{0,1:T(8,128)(2,1)S(1)} %get-tuple-element.254, s32[1024]{0:T(1024)S(1)} %fusion.90), kind=kCustom, calls=%fused_computation.2.clone.clone.1 | custom fusion | bytes 2101248 | tf_op jit(solution)/shard_map/while/body/eval_jaxpr/jit(_take)/gather | solution.py:17
  89.8 4.0 %gather_fusion.2 = bf16[1024,512]{1,0:T(8,128)(2,1)S(1)} fusion(bf16[512,2048]{0,1:T(8,128)(2,1)S(1)} %get-tuple-element.254, s32[1024]{0:T(1024)S(1)} %fusion.90), kind=kCustom, calls=%fused_computation.2.clone.clone.1 | custom fusion | bytes 2101248 | tf_op jit(solution)/shard_map/while/body/eval_jaxpr/jit(_take)/gather | solution.py:17
  96.3 4.0 %gather_fusion.2 = bf16[1024,512]{1,0:T(8,128)(2,1)S(1)} fusion(bf16[512,2048]{0,1:T(8,128)(2,1)S(1)} %get-tuple-element.254, s32[1024]{0:T(1024)S(1)} %fusion.90), kind=kCustom, calls=%fused_computation.2.clone.clone.1 | custom fusion | bytes 2101248 | tf_op jit(solution)/shard_map/while/body/eval_jaxpr/jit(_take)/gather | solution.py:17
  102.9 4.0 %gather_fusion.2 = bf16[1024,512]{1,0:T(8,128)(2,1)S(1)} fusion(bf16[512,2048]{0,1:T(8,128)(2,1)S(1)} %get-tuple-element.254, s32[1024]{0:T(1024)S(1)} %fusion.90), kind=kCustom, calls=%fused_computation.2.clone.clone.1 | custom fusion | bytes 2101248 | tf_op jit(solution)/shard_map/while/body/eval_jaxpr/jit(_take)/gather | solution.py:17
  109.5 4.0 %gather_fusion.2 = bf16[1024,512]{1,0:T(8,128)(2,1)S(1)} fusion(bf16[512,2048]{0,1:T(8,128)(2,1)S(1)} %get-tuple-element.254, s32[1024]{0:T(1024)S(1)} %fusion.90), kind=kCustom, calls=%fused_computation.2.clone.clone.1 | custom fusion | bytes 2101248 | tf_op jit(solution)/shard_map/while/body/eval_jaxpr/jit(_take)/gather | solution.py:17
  113.7 1.5 fusion.91
  116.1 4.0 %gather_fusion.2 = bf16[1024,512]{1,0:T(8,128)(2,1)S(1)} fusion(bf16[512,2048]{0,1:T(8,128)(2,1)S(1)} %get-tuple-element.254, s32[1024]{0:T(1024)S(1)} %fusion.90), kind=kCustom, calls=%fused_computation.2.clone.clone.1 | custom fusion | bytes 2101248 | tf_op jit(solution)/shard_map/while/body/eval_jaxpr/jit(_take)/gather | solution.py:17
  122.6 2.9 copy.14
  125.5 52.6 %while.20 = (s32[]{:T(128)}, f32[8,16,512]{2,1,0:T(8,128)S(1)}, s32[8,16,64]{2,1,0:T(8,128)S(1)}, bf16[512,2048]{0,1:T(8,128)(2,1)S(1)}, bf16[8,16,64]{2,1,0:T(8...) while((s32[]{:T(128)}, f32[8,16,512]{2,1,0:T(8,128)S(1)}, ...), condition=%wide.region_2.5_spmd, body=%wide.region_0.4_spmd.sunk | while | flops 70291552 | bytes 6755201 | solution.py:30
  126.3 4.0 %gather_fusion = bf16[1024,512]{1,0:T(8,128)(2,1)S(1)} fusion(bf16[512,2048]{0,1:T(8,128)(2,1)S(1)} %get-tuple-element.278, s32[1024]{0:T(1024)S(1)} %fusion.86), kind=kCustom, calls=%fused_computation.clone.clone.1 | custom fusion | bytes 2101248 | tf_op jit(solution)/shard_map/while/body/eval_jaxpr/jit(_take)/gather | solution.py:17
  130.4 1.5 fusion.87
  132.8 4.0 %gather_fusion = bf16[1024,512]{1,0:T(8,128)(2,1)S(1)} fusion(bf16[512,2048]{0,1:T(8,128)(2,1)S(1)} %get-tuple-element.278, s32[1024]{0:T(1024)S(1)} %fusion.86), kind=kCustom, calls=%fused_computation.clone.clone.1 | custom fusion | bytes 2101248 | tf_op jit(solution)/shard_map/while/body/eval_jaxpr/jit(_take)/gather | solution.py:17
  139.4 4.0 %gather_fusion = bf16[1024,512]{1,0:T(8,128)(2,1)S(1)} fusion(bf16[512,2048]{0,1:T(8,128)(2,1)S(1)} %get-tuple-element.278, s32[1024]{0:T(1024)S(1)} %fusion.86), kind=kCustom, calls=%fused_computation.clone.clone.1 | custom fusion | bytes 2101248 | tf_op jit(solution)/shard_map/while/body/eval_jaxpr/jit(_take)/gather | solution.py:17
  146.0 4.0 %gather_fusion = bf16[1024,512]{1,0:T(8,128)(2,1)S(1)} fusion(bf16[512,2048]{0,1:T(8,128)(2,1)S(1)} %get-tuple-element.278, s32[1024]{0:T(1024)S(1)} %fusion.86), kind=kCustom, calls=%fused_computation.clone.clone.1 | custom fusion | bytes 2101248 | tf_op jit(solution)/shard_map/while/body/eval_jaxpr/jit(_take)/gather | solution.py:17
  152.5 4.0 %gather_fusion = bf16[1024,512]{1,0:T(8,128)(2,1)S(1)} fusion(bf16[512,2048]{0,1:T(8,128)(2,1)S(1)} %get-tuple-element.278, s32[1024]{0:T(1024)S(1)} %fusion.86), kind=kCustom, calls=%fused_computation.clone.clone.1 | custom fusion | bytes 2101248 | tf_op jit(solution)/shard_map/while/body/eval_jaxpr/jit(_take)/gather | solution.py:17
  159.1 4.0 %gather_fusion = bf16[1024,512]{1,0:T(8,128)(2,1)S(1)} fusion(bf16[512,2048]{0,1:T(8,128)(2,1)S(1)} %get-tuple-element.278, s32[1024]{0:T(1024)S(1)} %fusion.86), kind=kCustom, calls=%fused_computation.clone.clone.1 | custom fusion | bytes 2101248 | tf_op jit(solution)/shard_map/while/body/eval_jaxpr/jit(_take)/gather | solution.py:17
  165.7 4.0 %gather_fusion = bf16[1024,512]{1,0:T(8,128)(2,1)S(1)} fusion(bf16[512,2048]{0,1:T(8,128)(2,1)S(1)} %get-tuple-element.278, s32[1024]{0:T(1024)S(1)} %fusion.86), kind=kCustom, calls=%fused_computation.clone.clone.1 | custom fusion | bytes 2101248 | tf_op jit(solution)/shard_map/while/body/eval_jaxpr/jit(_take)/gather | solution.py:17
  172.3 4.0 %gather_fusion = bf16[1024,512]{1,0:T(8,128)(2,1)S(1)} fusion(bf16[512,2048]{0,1:T(8,128)(2,1)S(1)} %get-tuple-element.278, s32[1024]{0:T(1024)S(1)} %fusion.86), kind=kCustom, calls=%fused_computation.clone.clone.1 | custom fusion | bytes 2101248 | tf_op jit(solution)/shard_map/while/body/eval_jaxpr/jit(_take)/gather | solution.py:17
  179.3 2.2 fusion.18
  183.9 112.4 %all-reduce.6.cloned.1.call-done = (f32[256,512]{1,0:T(8,128)}, f32[256,512]{1,0:T(8,128)}) async-done(((f32[256,512]{1,0:T(8,128)}, f32[256,512]{1,0:T(8,128)}), (f32[256,512]{1,0:T(8,128)}, f32[256,512]{1,0:T(8,128)})) %all-reduce.6.cloned.1.call-update) | async-done | bytes 1048592 | tf_op jit(solution)/shard_map/psum | solution.py:76
  298.5 30.7 %all-reduce.3 = (f32[17,17]{0,1:T(8,128)S(1)}, f32[17,8]{1,0:T(8,128)S(1)}, f32[17,17]{0,1:T(8,128)S(1)}, f32[17,8]{1,0:T(8,128)S(1)}) all-reduce(f32[17,17]{0,1:T(8,128)S(1)} %fusion.22, f32[17,8]{1,0:T(8,128)S(1)} %fusion.20, f32[17,17]{0,1:T(8,128)S(1)} %fusion.27, ...), channel_id=1, replica_groups=mesh['set'=32,'path'=8] {'path'}, use_global_device_ids=true, to_apply=%region_12.18 | all-reduce | flops 850 | bytes 6800 | tf_op jit(solution)/shard_map/psum | solution.py:80
  329.3 1.5 cholesky.55
  335.0 1.5 cholesky.44
  (230 shorter events, 53.0 us)
Async XLA Ops:
  7.2 5.4 %copy-start.4 = (f32[2048]{0:T(1024)S(1)}, f32[2048]{0:T(1024)}, u32[]{:S(2)}) copy-start(f32[2048]{0:T(1024)} %param.25) | copy-start | bytes 24580
  7.2 5.4 %copy-start.3 = (bf16[2,16,2048]{2,1,0:T(8,128)(2,1)S(1)}, bf16[2,16,2048]{2,1,0:T(8,128)(2,1)}, u32[]{:S(2)}) copy-start(bf16[2,16,2048]{2,1,0:T(8,128)(2,1)} %param.23) | copy-start | bytes 393220
  7.2 59.2 %all-gather.5.cloned.1.call-start = ((), (), s32[]{:S(2)}) async-start(), calls=%async_computation.1 | async-start | bytes 2162688 | tf_op jit(solution)/shard_map/all_gather | solution.py:67
  7.2 5.9 %copy-start = (bf16[2048,2048]{1,0:T(8,128)(2,1)S(1)}, bf16[2048,2048]{1,0:T(8,128)(2,1)}, u32[]{:S(2)}) copy-start(bf16[2048,2048]{1,0:T(8,128)(2,1)} %param.24) | copy-start | bytes 25165828
  13.1 2.7 copy-start.8
  13.1 2.8 copy-start.6
  13.1 2.9 copy-start.5
  13.1 3.0 copy-start.1
  15.0 106.9 %all-gather.3.cloned.1.call-start = ((), (), s32[]{:S(2)}) async-start(), calls=%async_computation | async-start | bytes 2162688 | tf_op jit(solution)/shard_map/all_gather | solution.py:67
  15.8 280.5 %all-reduce.6.cloned.1.call-start = ((), (), s32[]{:S(2)}) async-start(), calls=%async_computation.2 | async-start | bytes 2097152 | tf_op jit(solution)/shard_map/psum | solution.py:76
  121.9 0.7 copy-start.2
  125.5 52.6 %copy-start.7 = (s32[128]{0:T(128)S(1)}, s32[128]{0:T(128)}, u32[]{:S(2)}) copy-start(s32[128]{0:T(128)} %param.30) | copy-start | bytes 1540
Sparse Core Ops, SparseCore 0:
  15.2 51.1 all-gather.4
  68.9 47.9 all-gather.2
  181.6 114.6 all-reduce.5
where the time goes:
time: 350 us; the launch traced here: 348 us
  waiting for transfers between devices  159 us (45%)
  local copies, waits for them, and re-layouts  87.9 us (25%)
  matrix products  40.6 us (12%)
  blocking collectives  30.7 us (9%)
  other arithmetic  14.4 us (4%)
  between operations  14 us (4%)
    psum x1, waiting for transfers between devices, per_device(): summed = lax.psum(jnp.dot(onehot, values, precision=high), 'set')  112 us
    gather x16, local copies, waits for them, and re-layouts, value_block(): jnp.take(slab, lists_b.reshape(-1), axis=1)  63.4 us
    all_gather x2, waiting for transfers between devices, per_device(): piece = lax.all_gather(slab, 'set', axis=0, tiled=True)  45.7 us
    psum x1, blocking collectives, per_device(): lax.psum((jnp.dot(basis, basis.T, precision=high), jnp.dot(basis, netted....  30.7 us
    dot_general x16, matrix products, value_block(): jnp.einsum('psk,skl->psl', picked, gamma_b, preferred_element_type=jnp.fl...  24.4 us
    gather x16, local copies, waits for them, and re-layouts, value_block(): rates = jnp.exp(0.2 * jnp.take(slab, cur_b, axis=1).astype(jnp.float32))  9.44 us
    dot_general x2, matrix products, per_device(): jnp.dot(shocks[step], loading, preferred_element_type=jnp.float32)  7.25 us
  transfers between devices with their start and end apart: 3, of which 2 were waited for; matrix products, arithmetic and copies ran while one was open for 18% of the time, Pallas kernels for 0%

commit v1 on v0

v1 whole, which is shorter than its diff:
```python
import jax
import jax.numpy as jnp
from jax import lax
from jax.experimental import pallas as pl
from jax.experimental.pallas import tpu as pltpu
from jax.sharding import PartitionSpec as P

F32 = jnp.float32
BF16 = jnp.bfloat16
HIGH = lax.Precision.HIGHEST

NB = 16
STEPS = 2
ROWS = 16
LANES = 128
GRID = 4
HOPS = (0, 1, 3, 2)
NG = 4
PITCH = 9
SUB = 8
NBP = 24


def chip_index(y, x, core):
    return (y * GRID + x) * 2 + core


def hop_pairs(hop, flip):
    pairs = []
    for y in range(GRID):
        for x in range(GRID):
            for core in range(2):
                if core ^ flip == 0:
                    to = chip_index(y, (x + hop) % GRID, core)
                else:
                    to = chip_index((y + hop) % GRID, x, core)
                pairs.append((chip_index(y, x, core), to))
    return pairs


def core_pairs():
    return [(i, i ^ 1) for i in range(2 * GRID * GRID)]


def prepare(gamma, delta):
    sets, depth, _ = gamma.shape
    wide = NG * depth
    per = 4

    def body(g_ref, d_ref, o_ref):
        zero = jnp.zeros((depth, depth), F32)
        row = lax.broadcasted_iota(jnp.int32, (16, depth), 0)
        for b in range(per):
            for i in range(NG):
                j = b * NG + i
                g = g_ref[j].astype(F32) * 0.5
                parts = [g if k == i else zero for k in range(NG)]
                o_ref[b, i * depth:(i + 1) * depth, :] = jnp.concatenate(parts, axis=1).astype(BF16)
            d = [d_ref[b * NG + i:b * NG + i + 1, :].astype(F32) for i in range(NG)]
            tail = [jnp.where(row == i, jnp.broadcast_to(d[i], (16, depth)), 0.0) for i in range(NG)]
            o_ref[b, wide:, :] = jnp.concatenate(tail, axis=1).astype(BF16)

    return pl.pallas_call(
        body,
        grid=(sets // (NG * per),),
        in_specs=[
            pl.BlockSpec((NG * per, depth, depth), lambda i: (i, 0, 0)),
            pl.BlockSpec((NG * per, depth), lambda i: (i, 0)),
        ],
        out_specs=pl.BlockSpec((per, wide + 16, wide), lambda i: (i, 0, 0)),
        out_shape=jax.ShapeDtypeStruct((sets // NG, wide + 16, wide), BF16),
        name="prepare",
    )(gamma, delta)


def revalue(slots, lists, currency, owner, arrays, gd, sets, depth):
    factors = arrays[0].shape[1]
    blocks = arrays[0].shape[0] // (STEPS * ROWS)
    sources = len(arrays) * blocks
    chunks = sources * ROWS // LANES
    per_chunk = LANES // ROWS
    groups = sets // NG
    wide = NG * depth
    counterparties = 2 * 128
    tile = 256

    def body(slots, lists, cur, own, *refs):
        arrs = refs[:len(arrays)]
        gd_hbm, mine, theirs, base = refs[len(arrays):len(arrays) + 4]
        sl, st, xa, xb, rates, gdv, net, sem, gsem, osem = refs[len(arrays) + 4:]
        copies = []
        for a in range(len(arrays)):
            for e in range(blocks):
                n = a * blocks + e
                cp = pltpu.make_async_copy(
                    arrs[a].at[pl.ds(e * STEPS * ROWS, STEPS * ROWS), :], sl.at[slots[n]], sem.at[n]
                )
                cp.start()
                copies.append(cp)
        gcp = pltpu.make_async_copy(gd_hbm, gdv, gsem)
        gcp.start()
        net[...] = jnp.zeros(net.shape, F32)
        for cp in copies:
            cp.wait()

        def turn(ft, carry):
            f0 = pl.multiple_of(ft * tile, tile)
            for t in range(STEPS):
                for q in range(chunks):
                    blk = sl[pl.ds(per_chunk * q, per_chunk), pl.ds(t * ROWS, ROWS), pl.ds(f0, tile)]
                    o = jnp.transpose(blk.reshape(LANES, tile).astype(F32))
                    st[pl.ds(f0 * SUB + (t * chunks + q), tile, stride=SUB), :] = o
            return carry

        lax.fori_loop(0, factors // tile, turn, 0)
        for c in range(NB):
            b = st[pl.ds(c * SUB, SUB), :]
            base[pl.ds(c * SUB, SUB), :] = b
            rates[c] = jnp.exp(0.2 * b)

        def picks(j, x, k0, k1):
            for k in range(k0, k1):
                i = lists.at[pl.ds(k * groups, groups)][j]
                x[pl.ds(k * PITCH, SUB), :] = st[pl.ds(pl.multiple_of(i, SUB), SUB), :]

        sub = lax.broadcasted_iota(jnp.int32, (SUB, LANES), 0)
        halves = SUB // 2

        def value(j, x, jn, xn):
            g = gdv[j]
            loc = [jnp.zeros((SUB, LANES), F32) for _ in range(NG)]
            for p in range(halves):
                picks(jn, xn, wide * p // halves, wide * (p + 1) // halves)
                xs = jnp.concatenate(
                    [x[pl.ds(2 * p, wide, stride=PITCH), :], x[pl.ds(2 * p + 1, wide, stride=PITCH), :]], axis=1
                )
                o = jnp.dot(g, xs.astype(BF16), preferred_element_type=F32)
                for i in range(NG):
                    y = xs[i * depth:(i + 1) * depth] * o[i * depth:(i + 1) * depth]
                    r = jnp.sum(y, axis=0, keepdims=True) + o[wide + i:wide + i + 1]
                    loc[i] = jnp.where(sub == 2 * p, r[:, :LANES], loc[i])
                    loc[i] = jnp.where(sub == 2 * p + 1, r[:, LANES:], loc[i])
            for i in range(NG):
                s = j * NG + i
                c = own[s]
                net[c] = net[c] + loc[i] * rates[cur[s]]

        gcp.wait()
        picks(0, xa, 0, wide)

        def loop(jj, carry):
            j = jj * 2
            value(j, xa, j + 1, xb)
            value(j + 1, xb, jnp.minimum(j + 2, groups - 1), xa)
            return carry

        lax.fori_loop(0, groups // 2, loop, 0)
        half = counterparties // 2
        outs = [
            pltpu.make_async_copy(net.at[pl.ds(half, half)], theirs, osem.at[0]),
            pltpu.make_async_copy(net.at[pl.ds(0, half)], mine, osem.at[1]),
        ]
        for cp in outs:
            cp.start()
        for cp in outs:
            cp.wait()

    smem = pl.BlockSpec(memory_space=pltpu.SMEM)
    hbm = pl.BlockSpec(memory_space=pltpu.HBM)
    vmem = pl.BlockSpec(memory_space=pltpu.VMEM)
    half_shape = jax.ShapeDtypeStruct((counterparties // 2, SUB, LANES), F32)
    return pl.pallas_call(
        body,
        in_specs=[smem] * 4 + [hbm] * (len(arrays) + 1),
        out_specs=(hbm, hbm, vmem),
        out_shape=(half_shape, half_shape, jax.ShapeDtypeStruct((NB * SUB, LANES), F32)),
        scratch_shapes=[
            pltpu.VMEM((sources, STEPS * ROWS, factors), BF16),
            pltpu.VMEM((factors * SUB, LANES), F32),
            pltpu.VMEM((wide * PITCH, LANES), F32),
            pltpu.VMEM((wide * PITCH, LANES), F32),
            pltpu.VMEM((NB, SUB, LANES), F32),
            pltpu.VMEM(gd.shape, BF16),
            pltpu.VMEM((counterparties, SUB, LANES), F32),
            pltpu.SemaphoreType.DMA((sources,)),
            pltpu.SemaphoreType.DMA(()),
            pltpu.SemaphoreType.DMA((2,)),
        ],
        compiler_params=pltpu.CompilerParams(vmem_limit_bytes=40 * 1024 * 1024),
        name="revalue",
    )(slots, lists, currency, owner, *[pltpu.with_memory_space_constraint(a, pltpu.HBM) for a in (*arrays, gd)])


def basis_rows(base, s):
    row = lax.broadcasted_iota(jnp.int32, (NBP - NB, LANES), 0)
    one = jnp.where(row == 0, 1.0, 0.0).astype(F32)
    return jnp.concatenate([base[pl.ds(s, NB, stride=SUB), :], one], axis=0)


def moments_of(parts, base):
    chunks = SUB // STEPS

    def body(p_ref, b_ref, net_ref, out_ref):
        net_ref[...] = jnp.sum(p_ref[...], axis=0)
        out_ref[...] = jnp.zeros(out_ref.shape, F32)
        for t in range(STEPS):
            left, right = [], []
            for q in range(chunks):
                s = t * chunks + q
                b = basis_rows(b_ref, s)
                right.append(b)
                left.append(jnp.concatenate([b, net_ref[pl.ds(s, SUB, stride=SUB), :]], axis=0))
            m = lax.dot_general(
                jnp.concatenate(left, axis=1), jnp.concatenate(right, axis=1), (((1,), (1,)), ((), ())),
                precision=HIGH, preferred_element_type=F32,
            )
            out_ref[t, :, 0:NBP] = m

    return pl.pallas_call(
        body,
        out_shape=(
            jax.ShapeDtypeStruct((SUB * SUB, LANES), F32),
            jax.ShapeDtypeStruct((STEPS, NBP + SUB, LANES), F32),
        ),
        name="moments",
    )(parts, base)


def expose(payload, net, base, total):
    chunks = SUB // STEPS

    def body(p_ref, n_ref, b_ref, o_ref):
        acc = jnp.sum(p_ref[...], axis=0) * (1.0 / total)
        row = lax.broadcasted_iota(jnp.int32, (NBP + SUB, LANES), 0)
        lane = lax.broadcasted_iota(jnp.int32, (NBP + SUB, LANES), 1)
        diag = jnp.where((row == lane) & (row < NBP), jnp.where(row <= NB, 0.001, 1.0), 0.0)
        sys = [acc[t] + diag for t in range(STEPS)]
        for k in range(NB + 1):
            for t in range(STEPS):
                a = sys[t]
                r = a[k:k + 1, :]
                c = a[:, k:k + 1] / a[k:k + 1, k:k + 1]
                sys[t] = jnp.where(lane == k, c, a - c * r)
        for t in range(STEPS):
            coef = sys[t][NBP:, 0:NBP]
            for q in range(chunks):
                s = t * chunks + q
                fitted = jnp.dot(coef, basis_rows(b_ref, s), precision=HIGH, preferred_element_type=F32)
                n = n_ref[pl.ds(s, SUB, stride=SUB), :]
                o_ref[t, :, q * LANES:(q + 1) * LANES] = jnp.maximum(n - 0.9 * fitted, 0.0)

    return pl.pallas_call(
        body,
        out_shape=jax.ShapeDtypeStruct((STEPS, SUB, chunks * LANES), F32),
        name="expose",
    )(payload, net, base)


def per_device(start_state, shocks, loading, decay, factor_lists, delta, gamma, currency, owner):
    member = lax.axis_index("set")
    core, px, py = member % 2, (member // 2) % GRID, member // (2 * GRID)
    sets, depth = factor_lists.shape
    total = ROWS * lax.axis_size("set") * lax.axis_size("path")
    factors = start_state.shape[1]

    moved = jnp.dot(shocks.reshape(STEPS * ROWS, factors), loading, preferred_element_type=F32)
    first = decay[None, :] * start_state + moved[:ROWS]
    state = decay[None, :] * first + moved[ROWS:]
    slab = jnp.concatenate([first, state], axis=0).astype(BF16)

    line = [slab] + [lax.ppermute(slab, "set", hop_pairs(h, 0)) for h in HOPS[1:]]
    line = jnp.concatenate(line, axis=0)
    plane = [line] + [lax.ppermute(line, "set", hop_pairs(h, 1)) for h in HOPS[1:]]
    other = [lax.ppermute(a, "set", core_pairs()) for a in plane]

    hops = jnp.array(HOPS, jnp.int32)
    near, far = hops[None, :], hops[:, None]

    def slots_of(c):
        dx = jnp.where(c == 0, near, far)
        dy = jnp.where(c == 0, far, near)
        return (((py - dy) % GRID * GRID + (px - dx) % GRID) * 2 + c).reshape(-1)

    slots = jnp.concatenate([slots_of(core), slots_of(1 - core)]).astype(jnp.int32)
    lists = (factor_lists * SUB).reshape(sets // NG, NG * depth).T.reshape(-1)
    place = jnp.where((owner // SUB) % 2 == core, 0, 128) + owner // (2 * SUB) * SUB + owner % SUB

    gd = prepare(gamma, delta)
    mine, theirs, base = revalue(slots, lists, currency, place, plane + other, gd, sets, depth)
    mine = mine + lax.ppermute(theirs, "set", core_pairs())
    chips = [[i * 2 + c for i in range(GRID * GRID)] for c in range(2)]
    parts = lax.all_to_all(
        mine.reshape(GRID * GRID, SUB * SUB, LANES), "set", 0, 0, axis_index_groups=chips
    )
    net, payload = moments_of(parts, base)
    paths = lax.axis_size("path")
    payload = lax.all_to_all(jnp.broadcast_to(payload[None], (paths,) + payload.shape), "path", 0, 0)
    return expose(payload, net, base, total), state


def solution(mesh):
    return jax.shard_map(
        per_device,
        mesh=mesh,
        in_specs=(
            P(("path", "set"), None),
            P(None, ("path", "set"), None),
            P(),
            P(),
            P("set", None),
            P("set", None),
            P("set", None, None),
            P("set"),
            P("set"),
        ),
        out_specs=(P(None, "set", "path"), P(("path", "set"), None)),
        check_vma=False,
    )
```

time: 350 us -> 100 us (0.29)
  waiting for transfers between devices: 159 us -> 9.22 us
  local copies, waits for them, and re-layouts: 87.9 us -> 7.87 us
  matrix products: 40.6 us -> 5.01 us
  Pallas kernels: 0 us -> 30 us
  other arithmetic: 14.4 us -> 0.96 us
  between operations: 14 us -> 0.83 us
  starting transfers between devices: 0.12 us -> 10.6 us
  blocking collectives: 30.7 us -> 35.4 us
    psum x1 -> x0, waiting for transfers between devices: 112 us -> none  [per_device(): summed = lax.psum(jnp.dot(onehot, values, precision=high), 'set')]
    gather x32 -> x0, local copies, waits for them, and re-layouts: 72.9 us -> none  [the longest x16 63.4 us: value_block(): jnp.take(slab, lists_b.reshape(-1), axis=1)]
    all_gather x2 -> x0, waiting for transfers between devices: 45.7 us -> none  [per_device(): piece = lax.all_gather(slab, 'set', axis=0, tiled=True)]
    all_to_all x0 -> x2, blocking collectives: none -> 35.4 us  [the longest x1 18.1 us: per_device(): lax.all_to_all(jnp.broadcast_to(payload[None], (paths,) + payload.shape),...]
    dot_general x26 -> x1, matrix products: 39.9 us -> 5.01 us  [per_device(): jnp.dot(shocks.reshape(STEPS * ROWS, factors), loading, preferred_element...]
    psum x1 -> x0, blocking collectives: 30.7 us -> none  [per_device(): lax.psum((jnp.dot(basis, basis.T, precision=high), jnp.dot(basis, netted....]
    pallas_call x0 -> x4, Pallas kernels: none -> 30 us  [the longest x1 18.5 us: revalue(): pl.pallas_call(body, in_specs=[smem] * 4 + [hbm] * (len(arrays) + 1), out...]
    ppermute x0 -> x11, starting transfers between devices: none -> 10.6 us  [the longest x3 4.99 us: per_device(): lax.ppermute(line, 'set', hop_pairs(h, 1))]
  transfers between devices with their start and end apart: 3 -> 11, of which waited for: 2 -> 8; matrix products, arithmetic and copies ran while one was open for 18% -> 5% of each run, Pallas kernels for 0% -> 6%
where the time goes in v1:
time: 100 us
  blocking collectives  35.4 us (35%)
  Pallas kernels  30 us (30%)
  starting transfers between devices  10.6 us (11%)
  waiting for transfers between devices  9.22 us (9%)
  local copies, waits for them, and re-layouts  7.87 us (8%)
  matrix products  5.01 us (5%)
    pallas_call x1, Pallas kernels, revalue(): pl.pallas_call(body, in_specs=[smem] * 4 + [hbm] * (len(arrays) + 1), out...  18.5 us
    all_to_all x1, blocking collectives, per_device(): lax.all_to_all(jnp.broadcast_to(payload[None], (paths,) + payload.shape),...  18.1 us
    all_to_all x1, blocking collectives, per_device(): lax.all_to_all(mine.reshape(GRID * GRID, SUB * SUB, LANES), 'set', 0, 0,...  17.2 us
    unnamed x40, local copies, waits for them, and re-layouts  6.38 us
    pallas_call x1, Pallas kernels, prepare(): pl.pallas_call(body, grid=(sets // (NG * per),), in_specs=[pl.BlockSpec((...  6.38 us
    dot_general x1, matrix products, per_device(): jnp.dot(shocks.reshape(STEPS * ROWS, factors), loading, preferred_element...  5.01 us
    ppermute x3, starting transfers between devices, per_device(): lax.ppermute(line, 'set', hop_pairs(h, 1))  4.99 us
    ppermute x3, waiting for transfers between devices, per_device(): lax.ppermute(slab, 'set', hop_pairs(h, 0))  4.46 us
  transfers between devices with their start and end apart: 11, of which 8 were waited for; matrix products, arithmetic and copies ran while one was open for 5% of the time, Pallas kernels for 6%

profile of v1, /device:TPU:2, one launch (start us, length us, event | category | flops | bytes accessed | tf_op | source)
XLA Modules:
  0.0 100.0 jit_solution(3825406067932237394)
XLA Ops:
  0.7 0.9 copy-done
  1.6 5.0 %fusion.13 = f32[32,2048]{1,0:T(8,128)S(1)} fusion(bf16[32,2048]{1,0:T(8,128)(2,1)S(1)} %bitcast.5, bf16[2048,2048]{1,0:T(8,128)(2,1)} %param.12), kind=kOutput, calls=%fused_computation.52 | convolution fusion | flops 268435456 | bytes 8781824 | tf_op jit(solution)/shard_map/dot_general | solution.py:266
  6.6 0.7 constant_dynamic-update-slice_fusion.3
  7.3 1.6 %collective-permute-start = (bf16[32,2048]{1,0:T(8,128)(2,1)S(1)}, bf16[32,2048]{1,0:T(8,128)(2,1)S(1)}, u32[]{:S(2)}, u32[]{:S(2)}) collective-permute-start(bf16[32,2048]{1,0:T(8,128)(2,1)S(1)} %pad_maximum_fusion), channel_id=1, source_target_pairs={{0,16},{8,72},{16,32},{24,88},{32,48},{40,104},{48,0},{56,120},{64... | collective-permute-start | bytes 393224 | tf_op jit(solution)/shard_map/ppermute | solution.py:271
  8.9 0.8 collective-permute-start.1
  9.7 2.0 %collective-permute-start.2 = (bf16[32,2048]{1,0:T(8,128)(2,1)S(1)}, bf16[32,2048]{1,0:T(8,128)(2,1)S(1)}, u32[]{:S(2)}, u32[]{:S(2)}) collective-permute-start(bf16[32,2048]{1,0:T(8,128)(2,1)S(1)} %pad_maximum_fusion), channel_id=1, source_target_pairs={{0,32},{8,136},{16,48},{24,152},{32,0},{40,168},{48,16},{56,184},{... | collective-permute-start | bytes 393224 | tf_op jit(solution)/shard_map/ppermute | solution.py:271
  11.7 0.9 collective-permute-done
  12.6 1.3 %collective-permute-done.1 = bf16[32,2048]{1,0:T(8,128)(2,1)S(1)} collective-permute-done((bf16[32,2048]{1,0:T(8,128)(2,1)S(1)}, bf16[32,2048]{1,0:T(8,128)(2,1)S(1)}, u32[]{:S(2)}, u32[]{:S(2)}) %collective-permute-start.1) | collective-permute-done | bytes 131104 | tf_op jit(solution)/shard_map/ppermute | solution.py:271
  13.9 2.3 %collective-permute-done.2 = bf16[32,2048]{1,0:T(8,128)(2,1)S(1)} collective-permute-done((bf16[32,2048]{1,0:T(8,128)(2,1)S(1)}, bf16[32,2048]{1,0:T(8,128)(2,1)S(1)}, u32[]{:S(2)}, u32[]{:S(2)}) %collective-permute-start.2) | collective-permute-done | bytes 131104 | tf_op jit(solution)/shard_map/ppermute | solution.py:271
  16.2 1.3 %collective-permute-start.3 = (bf16[128,2048]{1,0:T(8,128)(2,1)S(1)}, bf16[128,2048]{1,0:T(8,128)(2,1)S(1)}, u32[]{:S(2)}, u32[]{:S(2)}) collective-permute-start(bf16[128,2048]{1,0:T(8,128)(2,1)S(1)} %constant_dynamic-update-slice_fusion.refs_0_), channel_id=1, source_target_pairs={{0,64},{8,24},{16,80},{24,40},{32,96},{40,56},{48,112},{56,8},{64,... | collective-permute-start | bytes 1572872 | tf_op jit(solution)/shard_map/ppermute | solution.py:273
  17.6 2.0 %collective-permute-start.4 = (bf16[128,2048]{1,0:T(8,128)(2,1)S(1)}, bf16[128,2048]{1,0:T(8,128)(2,1)S(1)}, u32[]{:S(2)}, u32[]{:S(2)}) collective-permute-start(bf16[128,2048]{1,0:T(8,128)(2,1)S(1)} %constant_dynamic-update-slice_fusion.refs_0_), channel_id=1, source_target_pairs={{0,192},{8,56},{16,208},{24,8},{32,224},{40,24},{48,240},{56,40},{... | collective-permute-start | bytes 1572872 | tf_op jit(solution)/shard_map/ppermute | solution.py:273
  19.6 1.7 %collective-permute-start.5 = (bf16[128,2048]{1,0:T(8,128)(2,1)S(1)}, bf16[128,2048]{1,0:T(8,128)(2,1)S(1)}, u32[]{:S(2)}, u32[]{:S(2)}) collective-permute-start(bf16[128,2048]{1,0:T(8,128)(2,1)S(1)} %constant_dynamic-update-slice_fusion.refs_0_), channel_id=1, source_target_pairs={{0,128},{8,40},{16,144},{24,56},{32,160},{40,8},{48,176},{56,24},{... | collective-permute-start | bytes 1572872 | tf_op jit(solution)/shard_map/ppermute | solution.py:273
  21.6 3.8 %copy.16.g_ref = bf16[128,64,64]{2,1,0:T(8,128)(2,1)} copy(bf16[128,64,64]{0,2,1:T(8,128)(2,1)S(1)} %copy-done.3) | data formatting | bytes 2097152 | tf_op args[6]
  25.4 0.7 copy.17.d_ref
  26.4 0.1 copy.15
  26.6 6.4 %prepare.1.refs_8_ = bf16[32,272,256]{2,1,0:T(8,128)(2,1)} custom-call(bf16[128,64,64]{2,1,0:T(8,128)(2,1)} %copy.16.g_ref, bf16[128,64]{1,0:T(8,128)(2,1)} %copy.17.d_ref), custom_call_target="tpu_custom_call" | custom-call | tf_op jit(solution)/shard_map/prepare/pallas_call | solution.py:63
  33.0 0.5 collective-permute-start.7
  33.5 0.1 collective-permute-start.8
  33.6 0.4 collective-permute-start.9
  34.1 0.8 collective-permute-done.6.refs_4_
  34.9 0.7 collective-permute-done.7.refs_5_
  35.6 0.7 collective-permute-done.8.refs_6_
  36.4 0.7 collective-permute-done.9.refs_7_
  37.2 0.8 copy-done.11
  38.0 18.5 %revalue.1 = (f32[128,8,128]{2,1,0:T(8,128)S(1)}, f32[128,8,128]{2,1,0:T(8,128)S(1)}, f32[128,128]{1,0:T(8,128)S(1)}) custom-call(s32[32]{0:T(128)S(1)} %pad_add_fusion.slots, s32[8192]{0:T(1024)S(1)} %reshape.47.lists, s32[128]{0:T(128)S(1)} %copy-done.2, s32[128]{0:T(128)S(1)} %fusion.3.own, bf16[128,2048]{1,0:T(8,128)(2,1)} %copy-done.4, ...), custom_call_target="tpu_custom_call" | custom-call | tf_op jit(solution)/shard_map/revalue/pallas_call | solution.py:172
  56.5 0.2 collective-permute-start.10
  56.8 1.8 %collective-permute-done.10 = f32[128,8,128]{2,1,0:T(8,128)S(1)} collective-permute-done((f32[128,8,128]{2,1,0:T(8,128)S(1)}, f32[128,8,128]{2,1,0:T(8,128)S(1)}, u32[]{:S(2)}, u32[]{:S(2)}) %collective-permute-start.10) | collective-permute-done | bytes 524320 | tf_op jit(solution)/shard_map/ppermute | solution.py:290
  58.6 17.2 %all_to_all.10.p_ref = f32[16,64,128]{2,1,0:T(8,128)} all-to-all(f32[16,64,128]{2,1,0:T(8,128)S(1)} %bitcast.6), channel_id=1, replica_groups={{0,16,32,48,64,80,96,112,128,144,160,176,192,208,224,240},{8,24,40,56,7..., dimensions={0} | all-to-all | bytes 1048576 | tf_op jit(solution)/shard_map/all_to_all | solution.py:292
  75.8 1.9 %moments.1 = (f32[64,128]{1,0:T(8,128)}, f32[2,32,128]{2,1,0:T(8,128)}) custom-call(f32[16,64,128]{2,1,0:T(8,128)} %all_to_all.10.p_ref, f32[128,128]{1,0:T(8,128)} %copy-done.1), custom_call_target="tpu_custom_call" | custom-call | tf_op jit(solution)/shard_map/moments/pallas_call | solution.py:219
  77.8 0.8 broadcast_in_dim.59
  78.6 18.1 %all_to_all.11.p_ref = f32[8,2,32,128]{3,2,1,0:T(8,128)} all-to-all(f32[8,2,32,128]{3,2,1,0:T(8,128)S(1)} %broadcast_in_dim.59), channel_id=1, replica_groups=mesh['set'=32,'path'=8] {'path'}, dimensions={0} | all-to-all | bytes 524288 | tf_op jit(solution)/shard_map/all_to_all | solution.py:297
  96.7 3.3 %expose.1 = f32[2,8,512]{2,1,0:T(8,128)} custom-call(f32[8,2,32,128]{3,2,1,0:T(8,128)} %all_to_all.11.p_ref, f32[64,128]{1,0:T(8,128)} %get-tuple-element.11.n_ref, f32[128,128]{1,0:T(8,128)} %copy-done.1), custom_call_target="tpu_custom_call" | custom-call | tf_op jit(solution)/shard_map/expose/pallas_call | solution.py:252
  (56 shorter events, 1.0 us)
Async XLA Ops:
  0.6 0.9 copy-start
  0.6 5.9 %copy-start.12 = (f32[16,2048]{1,0:T(8,128)S(1)}, f32[16,2048]{1,0:T(8,128)}, u32[]{:S(2)}) copy-start(f32[16,2048]{1,0:T(8,128)} %param.10) | copy-start | bytes 393220
  0.7 5.9 %copy-start.14 = (f32[2048]{0:T(1024)S(1)}, f32[2048]{0:T(1024)}, u32[]{:S(2)}) copy-start(f32[2048]{0:T(1024)} %param.13) | copy-start | bytes 24580
  1.5 19.7 %copy-start.16 = (s32[4]{0:T(128)S(1)}, s32[4]{0:T(128)}, u32[]{:S(2)}) copy-start(s32[4]{0:T(128)} %constant.119.clone) | copy-start | bytes 52
  1.5 20.1 %copy-start.3 = (bf16[128,64,64]{0,2,1:T(8,128)(2,1)S(1)}, bf16[128,64,64]{0,2,1:T(8,128)(2,1)}, u32[]{:S(2)}) copy-start(bf16[128,64,64]{0,2,1:T(8,128)(2,1)} %param.16) | copy-start | bytes 3145732
  1.5 23.9 %copy-start.15 = (bf16[128,64]{0,1:T(8,128)(2,1)S(1)}, bf16[128,64]{0,1:T(8,128)(2,1)}, u32[]{:S(2)}) copy-start(bf16[128,64]{0,1:T(8,128)(2,1)} %param.15) | copy-start | bytes 49156
  1.5 24.6 %copy-start.13 = (s32[128,64]{0,1:T(8,128)S(1)}, s32[128,64]{0,1:T(8,128)}, u32[]{:S(2)}) copy-start(s32[128,64]{0,1:T(8,128)} %param.14) | copy-start | bytes 98308
  6.6 27.5 %copy-start.17 = (s32[128]{0:T(128)S(1)}, s32[128]{0:T(128)}, u32[]{:S(2)}) copy-start(s32[128]{0:T(128)} %param.18) | copy-start | bytes 1540
  6.6 31.4 %copy-start.2 = (s32[128]{0:T(128)S(1)}, s32[128]{0:T(128)}, u32[]{:S(2)}) copy-start(s32[128]{0:T(128)} %cur.1) | copy-start | bytes 1540
  7.3 5.3 %collective-permute-start = (bf16[32,2048]{1,0:T(8,128)(2,1)S(1)}, bf16[32,2048]{1,0:T(8,128)(2,1)S(1)}, u32[]{:S(2)}, u32[]{:S(2)}) collective-permute-start(bf16[32,2048]{1,0:T(8,128)(2,1)S(1)} %pad_maximum_fusion), channel_id=1, source_target_pairs={{0,16},{8,72},{16,32},{24,88},{32,48},{40,104},{48,0},{56,120},{64... | collective-permute-start | bytes 393224 | tf_op jit(solution)/shard_map/ppermute | solution.py:271
  8.9 5.0 %collective-permute-start.1 = (bf16[32,2048]{1,0:T(8,128)(2,1)S(1)}, bf16[32,2048]{1,0:T(8,128)(2,1)S(1)}, u32[]{:S(2)}, u32[]{:S(2)}) collective-permute-start(bf16[32,2048]{1,0:T(8,128)(2,1)S(1)} %pad_maximum_fusion), channel_id=1, source_target_pairs={{0,48},{8,200},{16,0},{24,216},{32,16},{40,232},{48,32},{56,248},{... | collective-permute-start | bytes 393224 | tf_op jit(solution)/shard_map/ppermute | solution.py:271
  9.7 6.5 %collective-permute-start.2 = (bf16[32,2048]{1,0:T(8,128)(2,1)S(1)}, bf16[32,2048]{1,0:T(8,128)(2,1)S(1)}, u32[]{:S(2)}, u32[]{:S(2)}) collective-permute-start(bf16[32,2048]{1,0:T(8,128)(2,1)S(1)} %pad_maximum_fusion), channel_id=1, source_target_pairs={{0,32},{8,136},{16,48},{24,152},{32,0},{40,168},{48,16},{56,184},{... | collective-permute-start | bytes 393224 | tf_op jit(solution)/shard_map/ppermute | solution.py:271
  16.2 20.9 %copy-start.4 = (bf16[128,2048]{1,0:T(8,128)(2,1)}, bf16[128,2048]{1,0:T(8,128)(2,1)S(1)}, u32[]{:S(2)}) copy-start(bf16[128,2048]{1,0:T(8,128)(2,1)S(1)} %constant_dynamic-update-slice_fusion.refs_0_) | copy-start | bytes 1572868
  16.2 16.7 %collective-permute-start.3 = (bf16[128,2048]{1,0:T(8,128)(2,1)S(1)}, bf16[128,2048]{1,0:T(8,128)(2,1)S(1)}, u32[]{:S(2)}, u32[]{:S(2)}) collective-permute-start(bf16[128,2048]{1,0:T(8,128)(2,1)S(1)} %constant_dynamic-update-slice_fusion.refs_0_), channel_id=1, source_target_pairs={{0,64},{8,24},{16,80},{24,40},{32,96},{40,56},{48,112},{56,8},{64,... | collective-permute-start | bytes 1572872 | tf_op jit(solution)/shard_map/ppermute | solution.py:273
  17.6 15.9 %collective-permute-start.4 = (bf16[128,2048]{1,0:T(8,128)(2,1)S(1)}, bf16[128,2048]{1,0:T(8,128)(2,1)S(1)}, u32[]{:S(2)}, u32[]{:S(2)}) collective-permute-start(bf16[128,2048]{1,0:T(8,128)(2,1)S(1)} %constant_dynamic-update-slice_fusion.refs_0_), channel_id=1, source_target_pairs={{0,192},{8,56},{16,208},{24,8},{32,224},{40,24},{48,240},{56,40},{... | collective-permute-start | bytes 1572872 | tf_op jit(solution)/shard_map/ppermute | solution.py:273
  19.6 14.0 %collective-permute-start.5 = (bf16[128,2048]{1,0:T(8,128)(2,1)S(1)}, bf16[128,2048]{1,0:T(8,128)(2,1)S(1)}, u32[]{:S(2)}, u32[]{:S(2)}) collective-permute-start(bf16[128,2048]{1,0:T(8,128)(2,1)S(1)} %constant_dynamic-update-slice_fusion.refs_0_), channel_id=1, source_target_pairs={{0,128},{8,40},{16,144},{24,56},{32,160},{40,8},{48,176},{56,24},{... | collective-permute-start | bytes 1572872 | tf_op jit(solution)/shard_map/ppermute | solution.py:273
  32.9 1.9 %collective-permute-start.6 = (bf16[128,2048]{1,0:T(8,128)(2,1)S(1)}, bf16[128,2048]{1,0:T(8,128)(2,1)S(1)}, u32[]{:S(2)}, u32[]{:S(2)}) collective-permute-start(bf16[128,2048]{1,0:T(8,128)(2,1)S(1)} %constant_dynamic-update-slice_fusion.refs_0_), channel_id=1, source_target_pairs={{0,8},{8,0},{16,24},{24,16},{32,40},{40,32},{48,56},{56,48},{64,72... | collective-permute-start | bytes 1572872 | tf_op jit(solution)/shard_map/ppermute | solution.py:274
  33.0 4.2 %copy-start.5 = (bf16[128,2048]{1,0:T(8,128)(2,1)}, bf16[128,2048]{1,0:T(8,128)(2,1)S(1)}, u32[]{:S(2)}) copy-start(bf16[128,2048]{1,0:T(8,128)(2,1)S(1)} %collective-permute-done.3.refs_1_) | copy-start | bytes 1572868
  33.0 2.6 %collective-permute-start.7 = (bf16[128,2048]{1,0:T(8,128)(2,1)S(1)}, bf16[128,2048]{1,0:T(8,128)(2,1)S(1)}, u32[]{:S(2)}, u32[]{:S(2)}) collective-permute-start(bf16[128,2048]{1,0:T(8,128)(2,1)S(1)} %collective-permute-done.3.refs_1_), channel_id=1, source_target_pairs={{0,8},{8,0},{16,24},{24,16},{32,40},{40,32},{48,56},{56,48},{64,72... | collective-permute-start | bytes 1572872 | tf_op jit(solution)/shard_map/ppermute | solution.py:274
  33.5 3.6 %copy-start.6 = (bf16[128,2048]{1,0:T(8,128)(2,1)}, bf16[128,2048]{1,0:T(8,128)(2,1)S(1)}, u32[]{:S(2)}) copy-start(bf16[128,2048]{1,0:T(8,128)(2,1)S(1)} %collective-permute-done.4.refs_2_) | copy-start | bytes 1572868
  33.5 2.9 %collective-permute-start.8 = (bf16[128,2048]{1,0:T(8,128)(2,1)S(1)}, bf16[128,2048]{1,0:T(8,128)(2,1)S(1)}, u32[]{:S(2)}, u32[]{:S(2)}) collective-permute-start(bf16[128,2048]{1,0:T(8,128)(2,1)S(1)} %collective-permute-done.4.refs_2_), channel_id=1, source_target_pairs={{0,8},{8,0},{16,24},{24,16},{32,40},{40,32},{48,56},{56,48},{64,72... | collective-permute-start | bytes 1572872 | tf_op jit(solution)/shard_map/ppermute | solution.py:274
  33.6 3.5 %copy-start.7 = (bf16[128,2048]{1,0:T(8,128)(2,1)}, bf16[128,2048]{1,0:T(8,128)(2,1)S(1)}, u32[]{:S(2)}) copy-start(bf16[128,2048]{1,0:T(8,128)(2,1)S(1)} %collective-permute-done.5.refs_3_) | copy-start | bytes 1572868
  33.6 3.5 %collective-permute-start.9 = (bf16[128,2048]{1,0:T(8,128)(2,1)S(1)}, bf16[128,2048]{1,0:T(8,128)(2,1)S(1)}, u32[]{:S(2)}, u32[]{:S(2)}) collective-permute-start(bf16[128,2048]{1,0:T(8,128)(2,1)S(1)} %collective-permute-done.5.refs_3_), channel_id=1, source_target_pairs={{0,8},{8,0},{16,24},{24,16},{32,40},{40,32},{48,56},{56,48},{64,72... | collective-permute-start | bytes 1572872 | tf_op jit(solution)/shard_map/ppermute | solution.py:274
  34.9 2.3 %copy-start.8 = (bf16[128,2048]{1,0:T(8,128)(2,1)}, bf16[128,2048]{1,0:T(8,128)(2,1)S(1)}, u32[]{:S(2)}) copy-start(bf16[128,2048]{1,0:T(8,128)(2,1)S(1)} %collective-permute-done.6.refs_4_) | copy-start | bytes 1572868
  35.6 1.5 %copy-start.9 = (bf16[128,2048]{1,0:T(8,128)(2,1)}, bf16[128,2048]{1,0:T(8,128)(2,1)S(1)}, u32[]{:S(2)}) copy-start(bf16[128,2048]{1,0:T(8,128)(2,1)S(1)} %collective-permute-done.7.refs_5_) | copy-start | bytes 1572868
  36.4 0.8 copy-start.10
  37.2 0.8 copy-start.11
  56.5 2.1 %copy-start.1 = (f32[128,128]{1,0:T(8,128)}, f32[128,128]{1,0:T(8,128)S(1)}, u32[]{:S(2)}) copy-start(f32[128,128]{1,0:T(8,128)S(1)} %get-tuple-element.9.b_ref) | copy-start | bytes 196612
  56.5 2.0 %collective-permute-start.10 = (f32[128,8,128]{2,1,0:T(8,128)S(1)}, f32[128,8,128]{2,1,0:T(8,128)S(1)}, u32[]{:S(2)}, u32[]{:S(2)}) collective-permute-start(f32[128,8,128]{2,1,0:T(8,128)S(1)} %get-tuple-element.8), channel_id=1, source_target_pairs={{0,8},{8,0},{16,24},{24,16},{32,40},{40,32},{48,56},{56,48},{64,72... | collective-permute-start | bytes 1572872 | tf_op jit(solution)/shard_map/ppermute | solution.py:290

commit v2 on v1

--- a/solution.py
+++ b/solution.py
@@ -18,7 +18,12 @@
 NG = 4
 PITCH = 9
 SUB = 8
+VMEM_SPEC = pl.BlockSpec(memory_space=pltpu.VMEM)
 NBP = 24
+
+
+def on_chip(a):
+    return pltpu.with_memory_space_constraint(a, pltpu.VMEM)
 
 
 def chip_index(y, x, core):
@@ -45,7 +50,7 @@
 def prepare(gamma, delta):
     sets, depth, _ = gamma.shape
     wide = NG * depth
-    per = 4
+    per = 16
 
     def body(g_ref, d_ref, o_ref):
         zero = jnp.zeros((depth, depth), F32)
@@ -87,21 +92,13 @@
     def body(slots, lists, cur, own, *refs):
         arrs = refs[:len(arrays)]
         gd_hbm, mine, theirs, base = refs[len(arrays):len(arrays) + 4]
-        sl, st, xa, xb, rates, gdv, net, sem, gsem, osem = refs[len(arrays) + 4:]
-        copies = []
-        for a in range(len(arrays)):
-            for e in range(blocks):
-                n = a * blocks + e
-                cp = pltpu.make_async_copy(
-                    arrs[a].at[pl.ds(e * STEPS * ROWS, STEPS * ROWS), :], sl.at[slots[n]], sem.at[n]
-                )
-                cp.start()
-                copies.append(cp)
+        sl, st, xa, xb, rates, gdv, net, gsem = refs[len(arrays) + 4:]
         gcp = pltpu.make_async_copy(gd_hbm, gdv, gsem)
         gcp.start()
         net[...] = jnp.zeros(net.shape, F32)
-        for cp in copies:
-            cp.wait()
+        for a in range(len(arrays)):
+            for e in range(blocks):
+                sl[slots[a * blocks + e]] = arrs[a][e * STEPS * ROWS:(e + 1) * STEPS * ROWS, :]
 
         def turn(ft, carry):
             f0 = pl.multiple_of(ft * tile, tile)
@@ -130,16 +127,20 @@
             g = gdv[j]
             loc = [jnp.zeros((SUB, LANES), F32) for _ in range(NG)]
             for p in range(halves):
-                picks(jn, xn, wide * p // halves, wide * (p + 1) // halves)
+                k0, k1 = wide * p // halves, wide * (p + 1) // halves
+                picks(jn, xn, k0, (k0 + k1) // 2)
                 xs = jnp.concatenate(
                     [x[pl.ds(2 * p, wide, stride=PITCH), :], x[pl.ds(2 * p + 1, wide, stride=PITCH), :]], axis=1
                 )
                 o = jnp.dot(g, xs.astype(BF16), preferred_element_type=F32)
+                picks(jn, xn, (k0 + k1) // 2, k1)
                 for i in range(NG):
-                    y = xs[i * depth:(i + 1) * depth] * o[i * depth:(i + 1) * depth]
-                    r = jnp.sum(y, axis=0, keepdims=True) + o[wide + i:wide + i + 1]
-                    loc[i] = jnp.where(sub == 2 * p, r[:, :LANES], loc[i])
-                    loc[i] = jnp.where(sub == 2 * p + 1, r[:, LANES:], loc[i])
+                    for h in range(2):
+                        lanes = slice(h * LANES, (h + 1) * LANES)
+                        again = x[pl.ds(i * depth * PITCH + 2 * p + h, depth, stride=PITCH), :]
+                        y = again * o[i * depth:(i + 1) * depth, lanes]
+                        r = jnp.sum(y, axis=0, keepdims=True) + o[wide + i:wide + i + 1, lanes]
+                        loc[i] = jnp.where(sub == 2 * p + h, r, loc[i])
             for i in range(NG):
                 s = j * NG + i
                 c = own[s]
@@ -156,24 +157,18 @@
 
         lax.fori_loop(0, groups // 2, loop, 0)
         half = counterparties // 2
-        outs = [
-            pltpu.make_async_copy(net.at[pl.ds(half, half)], theirs, osem.at[0]),
-            pltpu.make_async_copy(net.at[pl.ds(0, half)], mine, osem.at[1]),
-        ]
-        for cp in outs:
-            cp.start()
-        for cp in outs:
-            cp.wait()
+        theirs[...] = net[pl.ds(half, half)]
+        mine[...] = net[pl.ds(0, half)]
 
     smem = pl.BlockSpec(memory_space=pltpu.SMEM)
     hbm = pl.BlockSpec(memory_space=pltpu.HBM)
     vmem = pl.BlockSpec(memory_space=pltpu.VMEM)
-    half_shape = jax.ShapeDtypeStruct((counterparties // 2, SUB, LANES), F32)
-    return pl.pallas_call(
-        body,
-        in_specs=[smem] * 4 + [hbm] * (len(arrays) + 1),
-        out_specs=(hbm, hbm, vmem),
-        out_shape=(half_shape, half_shape, jax.ShapeDtypeStruct((NB * SUB, LANES), F32)),
+    half_shape = pltpu.VMEM((counterparties // 2, SUB, LANES), F32)
+    return pl.pallas_call(
+        body,
+        in_specs=[smem] * 4 + [vmem] * len(arrays) + [hbm],
+        out_specs=(vmem, vmem, vmem),
+        out_shape=(half_shape, half_shape, pltpu.VMEM((NB * SUB, LANES), F32)),
         scratch_shapes=[
             pltpu.VMEM((sources, STEPS * ROWS, factors), BF16),
             pltpu.VMEM((factors * SUB, LANES), F32),
@@ -182,13 +177,15 @@
             pltpu.VMEM((NB, SUB, LANES), F32),
             pltpu.VMEM(gd.shape, BF16),
             pltpu.VMEM((counterparties, SUB, LANES), F32),
-            pltpu.SemaphoreType.DMA((sources,)),
             pltpu.SemaphoreType.DMA(()),
-            pltpu.SemaphoreType.DMA((2,)),
         ],
         compiler_params=pltpu.CompilerParams(vmem_limit_bytes=40 * 1024 * 1024),
         name="revalue",
-    )(slots, lists, currency, owner, *[pltpu.with_memory_space_constraint(a, pltpu.HBM) for a in (*arrays, gd)])
+    )(
+        slots, lists, currency, owner,
+        *[on_chip(a) for a in arrays],
+        pltpu.with_memory_space_constraint(gd, pltpu.HBM),
+    )
 
 
 def basis_rows(base, s):
@@ -197,33 +194,42 @@
     return jnp.concatenate([base[pl.ds(s, NB, stride=SUB), :], one], axis=0)
 
 
-def moments_of(parts, base):
+def moments_of(parts, base, paths):
     chunks = SUB // STEPS
 
     def body(p_ref, b_ref, net_ref, out_ref):
         net_ref[...] = jnp.sum(p_ref[...], axis=0)
-        out_ref[...] = jnp.zeros(out_ref.shape, F32)
+        pad = jnp.zeros((LANES - NBP, chunks * LANES), F32)
+        m = []
         for t in range(STEPS):
-            left, right = [], []
+            right, mine = [], []
             for q in range(chunks):
                 s = t * chunks + q
-                b = basis_rows(b_ref, s)
-                right.append(b)
-                left.append(jnp.concatenate([b, net_ref[pl.ds(s, SUB, stride=SUB), :]], axis=0))
-            m = lax.dot_general(
-                jnp.concatenate(left, axis=1), jnp.concatenate(right, axis=1), (((1,), (1,)), ((), ())),
+                right.append(basis_rows(b_ref, s))
+                mine.append(net_ref[pl.ds(s, SUB, stride=SUB), :])
+            right = jnp.concatenate(right, axis=1)
+            left = jnp.concatenate([right, jnp.concatenate(mine, axis=1)], axis=0)
+            m.append(lax.dot_general(
+                left, jnp.concatenate([right, pad], axis=0), (((1,), (1,)), ((), ())),
                 precision=HIGH, preferred_element_type=F32,
-            )
-            out_ref[t, :, 0:NBP] = m
-
-    return pl.pallas_call(
-        body,
+            ))
+        low = jnp.concatenate([
+            pltpu.roll(m[t][NBP:], 2 * NBP, 1) + pltpu.roll(m[t][NB:NBP], 3 * NBP, 1) for t in range(STEPS)
+        ], axis=0)
+        packed = m[0][:NB] + pltpu.roll(m[1][:NB], NBP, 1) + low
+        for d in range(paths):
+            out_ref[d] = packed
+
+    return pl.pallas_call(
+        body,
+        in_specs=[VMEM_SPEC] * 2,
+        out_specs=(VMEM_SPEC, VMEM_SPEC),
         out_shape=(
-            jax.ShapeDtypeStruct((SUB * SUB, LANES), F32),
-            jax.ShapeDtypeStruct((STEPS, NBP + SUB, LANES), F32),
+            pltpu.VMEM((SUB * SUB, LANES), F32),
+            pltpu.VMEM((paths, NB, LANES), F32),
         ),
         name="moments",
-    )(parts, base)
+    )(on_chip(parts), on_chip(base))
 
 
 def expose(payload, net, base, total):
@@ -233,13 +239,21 @@
         acc = jnp.sum(p_ref[...], axis=0) * (1.0 / total)
         row = lax.broadcasted_iota(jnp.int32, (NBP + SUB, LANES), 0)
         lane = lax.broadcasted_iota(jnp.int32, (NBP + SUB, LANES), 1)
-        diag = jnp.where((row == lane) & (row < NBP), jnp.where(row <= NB, 0.001, 1.0), 0.0)
-        sys = [acc[t] + diag for t in range(STEPS)]
+        diag = jnp.where((row == lane) & (row <= NB), 0.001, 0.0)
+        sys = []
+        for t in range(STEPS):
+            rest = acc[t * SUB:(t + 1) * SUB]
+            a = jnp.concatenate([
+                acc if t == 0 else pltpu.roll(acc, LANES - NBP, 1),
+                pltpu.roll(rest, LANES - 3 * NBP, 1),
+                pltpu.roll(rest, LANES - 2 * NBP, 1),
+            ], axis=0)
+            sys.append(jnp.where(lane < NBP, a, 0.0) + diag)
         for k in range(NB + 1):
             for t in range(STEPS):
                 a = sys[t]
                 r = a[k:k + 1, :]
-                c = a[:, k:k + 1] / a[k:k + 1, k:k + 1]
+                c = a[:, k:k + 1] * (1.0 / a[k:k + 1, k:k + 1])
                 sys[t] = jnp.where(lane == k, c, a - c * r)
         for t in range(STEPS):
             coef = sys[t][NBP:, 0:NBP]
@@ -251,9 +265,66 @@
 
     return pl.pallas_call(
         body,
+        in_specs=[VMEM_SPEC] * 3,
+        out_specs=VMEM_SPEC,
         out_shape=jax.ShapeDtypeStruct((STEPS, SUB, chunks * LANES), F32),
         name="expose",
-    )(payload, net, base)
+    )(on_chip(payload), on_chip(net), on_chip(base))
+
+
+def evolve(start_state, shocks, loading, decay):
+    rows, factors = start_state.shape
+    parts = 8
+    deep = factors // parts
+
+    def body(z_hbm, l_hbm, s_hbm, d_hbm, slab_ref, end_ref, z, l, s, d, sem, lsem):
+        small = [
+            pltpu.make_async_copy(z_hbm, z, sem.at[0]),
+            pltpu.make_async_copy(s_hbm, s, sem.at[1]),
+            pltpu.make_async_copy(d_hbm, d, sem.at[2]),
+        ]
+        large = [
+            pltpu.make_async_copy(l_hbm.at[pl.ds(i * deep, deep)], l.at[pl.ds(i * deep, deep)], lsem.at[i])
+            for i in range(parts)
+        ]
+        for cp in small[:1] + large + small[1:]:
+            cp.start()
+        small[0].wait()
+        moved = jnp.zeros((STEPS * rows, factors), F32)
+        for i in range(parts):
+            large[i].wait()
+            moved = moved + jnp.dot(
+                z[:, i * deep:(i + 1) * deep], l[pl.ds(i * deep, deep), :], preferred_element_type=F32
+            )
+        for cp in small[1:]:
+            cp.wait()
+        first = d[...] * s[...] + moved[:rows]
+        end = d[...] * first + moved[rows:]
+        end_ref[...] = end
+        slab_ref[...] = jnp.concatenate([first, end], axis=0).astype(BF16)
+
+    hbm = pl.BlockSpec(memory_space=pltpu.HBM)
+    vmem = pl.BlockSpec(memory_space=pltpu.VMEM)
+    args = (shocks.reshape(STEPS * rows, factors), loading, start_state, decay.reshape(1, factors))
+    return pl.pallas_call(
+        body,
+        in_specs=[hbm] * 4,
+        out_specs=(vmem, vmem),
+        out_shape=(
+            pltpu.VMEM((STEPS * rows, factors), BF16),
+            jax.ShapeDtypeStruct((rows, factors), F32),
+        ),
+        scratch_shapes=[
+            pltpu.VMEM((STEPS * rows, factors), BF16),
+            pltpu.VMEM((factors, factors), BF16),
+            pltpu.VMEM((rows, factors), F32),
+            pltpu.VMEM((1, factors), F32),
+            pltpu.SemaphoreType.DMA((3,)),
+            pltpu.SemaphoreType.DMA((parts,)),
+        ],
+        compiler_params=pltpu.CompilerParams(vmem_limit_bytes=24 * 1024 * 1024),
+        name="evolve",
+    )(*[pltpu.with_memory_space_constraint(a, pltpu.HBM) for a in args])
 
 
 def per_device(start_state, shocks, loading, decay, factor_lists, delta, gamma, currency, owner):
@@ -261,12 +332,7 @@
     core, px, py = member % 2, (member // 2) % GRID, member // (2 * GRID)
     sets, depth = factor_lists.shape
     total = ROWS * lax.axis_size("set") * lax.axis_size("path")
-    factors = start_state.shape[1]
-
-    moved = jnp.dot(shocks.reshape(STEPS * ROWS, factors), loading, preferred_element_type=F32)
-    first = decay[None, :] * start_state + moved[:ROWS]
-    state = decay[None, :] * first + moved[ROWS:]
-    slab = jnp.concatenate([first, state], axis=0).astype(BF16)
+    slab, state = evolve(start_state, shocks, loading, decay)
 
     line = [slab] + [lax.ppermute(slab, "set", hop_pairs(h, 0)) for h in HOPS[1:]]
     line = jnp.concatenate(line, axis=0)
@@ -292,9 +358,8 @@
     parts = lax.all_to_all(
         mine.reshape(GRID * GRID, SUB * SUB, LANES), "set", 0, 0, axis_index_groups=chips
     )
-    net, payload = moments_of(parts, base)
-    paths = lax.axis_size("path")
-    payload = lax.all_to_all(jnp.broadcast_to(payload[None], (paths,) + payload.shape), "path", 0, 0)
+    net, payload = moments_of(parts, base, lax.axis_size("path"))
+    payload = lax.all_to_all(payload, "path", 0, 0)
     return expose(payload, net, base, total), state
 
 

time: 100 us -> 87.2 us (0.87)
  matrix products: 5.01 us -> 0 us
  Pallas kernels: 30 us -> 26.2 us
  local copies, waits for them, and re-layouts: 7.87 us -> 5.32 us
  blocking collectives: 35.4 us -> 33.9 us
  waiting for transfers between devices: 9.22 us -> 10.5 us
    dot_general x1 -> x0, matrix products: 5.01 us -> none  [per_device(): jnp.dot(shocks.reshape(STEPS * ROWS, factors), loading, preferred_element...]
    pallas_call x1, Pallas kernels: 6.38 us -> 3.7 us  [prepare(): pl.pallas_call(body, grid=(sets // (NG * per),), in_specs=[pl.BlockSpec((...]
    all_to_all x1, blocking collectives: 18.1 us -> 15.6 us  [per_device(): payload = lax.all_to_all(payload, 'path', 0, 0)]
    ppermute x3, waiting for transfers between devices: 0.01 us -> 2.44 us  [per_device(): lax.ppermute(line, 'set', hop_pairs(h, 1))]
    unnamed x40 -> x17, local copies, waits for them, and re-layouts: 6.38 us -> 4.61 us
    ppermute x4, waiting for transfers between devices: 3 us -> 1.77 us  [per_device(): other = [lax.ppermute(a, 'set', core_pairs()) for a in plane]]
    pallas_call x3 -> x4, Pallas kernels: 23.7 us -> 22.5 us  [the longest x1 14.8 us: revalue(): pl.pallas_call(body, in_specs=[smem] * 4 + [vmem] * len(arrays) + [hbm],...]
    all_to_all x1, blocking collectives: 17.2 us -> 18.3 us  [per_device(): lax.all_to_all(mine.reshape(GRID * GRID, SUB * SUB, LANES), 'set', 0, 0,...]
  transfers between devices with their start and end apart: 11 -> 11, of which waited for: 8 -> 8; matrix products, arithmetic and copies ran while one was open for 5% -> 6% of each run, Pallas kernels for 6% -> 4%
where the time goes in v2:
time: 87.2 us; the launch traced here: 87 us
  blocking collectives  33.9 us (39%)
  Pallas kernels  26.2 us (30%)
  waiting for transfers between devices  10.5 us (12%)
  starting transfers between devices  10.1 us (12%)
  local copies, waits for them, and re-layouts  5.32 us (6%)
    all_to_all x1, blocking collectives, per_device(): lax.all_to_all(mine.reshape(GRID * GRID, SUB * SUB, LANES), 'set', 0, 0,...  18.3 us
    all_to_all x1, blocking collectives, per_device(): payload = lax.all_to_all(payload, 'path', 0, 0)  15.6 us
    pallas_call x1, Pallas kernels, revalue(): pl.pallas_call(body, in_specs=[smem] * 4 + [vmem] * len(arrays) + [hbm],...  14.8 us
    pallas_call x1, Pallas kernels, evolve(): pl.pallas_call(body, in_specs=[hbm] * 4, out_specs=(vmem, vmem), out_shap...  5.01 us
    ppermute x3, starting transfers between devices, per_device(): lax.ppermute(line, 'set', hop_pairs(h, 1))  4.99 us
    unnamed x17, local copies, waits for them, and re-layouts  4.61 us
    ppermute x3, waiting for transfers between devices, per_device(): lax.ppermute(slab, 'set', hop_pairs(h, 0))  4.45 us
    ppermute x3, starting transfers between devices, per_device(): lax.ppermute(slab, 'set', hop_pairs(h, 0))  4.39 us
  transfers between devices with their start and end apart: 11, of which 8 were waited for; matrix products, arithmetic and copies ran while one was open for 6% of the time, Pallas kernels for 4%

profile of v2, /device:TPU:2, one launch (start us, length us, event | category | flops | bytes accessed | tf_op | source)
XLA Modules:
  0.0 87.0 jit_solution(14185621553175860154)
XLA Ops:
  0.7 5.0 %evolve.1 = (bf16[32,2048]{1,0:T(8,128)(2,1)S(1)}, f32[16,2048]{1,0:T(8,128)}) custom-call(bf16[32,2048]{1,0:T(8,128)(2,1)} %bitcast.5, bf16[2048,2048]{1,0:T(8,128)(2,1)} %l_hbm.1, f32[16,2048]{1,0:T(8,128)} %s_hbm.1, f32[1,2048]{1,0:T(1,128)} %bitcast.7), custom_call_target="tpu_custom_call" | custom-call | tf_op jit(solution)/shard_map/evolve/pallas_call | solution.py:309
  5.7 1.6 %collective-permute-start = (bf16[32,2048]{1,0:T(8,128)(2,1)S(1)}, bf16[32,2048]{1,0:T(8,128)(2,1)S(1)}, u32[]{:S(2)}, u32[]{:S(2)}) collective-permute-start(bf16[32,2048]{1,0:T(8,128)(2,1)S(1)} %get-tuple-element.9), channel_id=1, source_target_pairs={{0,16},{8,72},{16,32},{24,88},{32,48},{40,104},{48,0},{56,120},{64... | collective-permute-start | bytes 393224 | tf_op jit(solution)/shard_map/ppermute | solution.py:337
  7.3 0.8 collective-permute-start.1
  8.1 2.0 %collective-permute-start.2 = (bf16[32,2048]{1,0:T(8,128)(2,1)S(1)}, bf16[32,2048]{1,0:T(8,128)(2,1)S(1)}, u32[]{:S(2)}, u32[]{:S(2)}) collective-permute-start(bf16[32,2048]{1,0:T(8,128)(2,1)S(1)} %get-tuple-element.9), channel_id=1, source_target_pairs={{0,32},{8,136},{16,48},{24,152},{32,0},{40,168},{48,16},{56,184},{... | collective-permute-start | bytes 393224 | tf_op jit(solution)/shard_map/ppermute | solution.py:337
  10.1 0.9 collective-permute-done
  11.0 1.3 %collective-permute-done.1 = bf16[32,2048]{1,0:T(8,128)(2,1)S(1)} collective-permute-done((bf16[32,2048]{1,0:T(8,128)(2,1)S(1)}, bf16[32,2048]{1,0:T(8,128)(2,1)S(1)}, u32[]{:S(2)}, u32[]{:S(2)}) %collective-permute-start.1) | collective-permute-done | bytes 131104 | tf_op jit(solution)/shard_map/ppermute | solution.py:337
  12.2 2.3 %collective-permute-done.2 = bf16[32,2048]{1,0:T(8,128)(2,1)S(1)} collective-permute-done((bf16[32,2048]{1,0:T(8,128)(2,1)S(1)}, bf16[32,2048]{1,0:T(8,128)(2,1)S(1)}, u32[]{:S(2)}, u32[]{:S(2)}) %collective-permute-start.2) | collective-permute-done | bytes 131104 | tf_op jit(solution)/shard_map/ppermute | solution.py:337
  14.6 1.3 %collective-permute-start.3 = (bf16[128,2048]{1,0:T(8,128)(2,1)S(1)}, bf16[128,2048]{1,0:T(8,128)(2,1)S(1)}, u32[]{:S(2)}, u32[]{:S(2)}) collective-permute-start(bf16[128,2048]{1,0:T(8,128)(2,1)S(1)} %constant_dynamic-update-slice_fusion.refs_0_), channel_id=1, source_target_pairs={{0,64},{8,24},{16,80},{24,40},{32,96},{40,56},{48,112},{56,8},{64,... | collective-permute-start | bytes 1572872 | tf_op jit(solution)/shard_map/ppermute | solution.py:339
  15.9 2.0 %collective-permute-start.4 = (bf16[128,2048]{1,0:T(8,128)(2,1)S(1)}, bf16[128,2048]{1,0:T(8,128)(2,1)S(1)}, u32[]{:S(2)}, u32[]{:S(2)}) collective-permute-start(bf16[128,2048]{1,0:T(8,128)(2,1)S(1)} %constant_dynamic-update-slice_fusion.refs_0_), channel_id=1, source_target_pairs={{0,192},{8,56},{16,208},{24,8},{32,224},{40,24},{48,240},{56,40},{... | collective-permute-start | bytes 1572872 | tf_op jit(solution)/shard_map/ppermute | solution.py:339
  17.9 1.7 %collective-permute-start.5 = (bf16[128,2048]{1,0:T(8,128)(2,1)S(1)}, bf16[128,2048]{1,0:T(8,128)(2,1)S(1)}, u32[]{:S(2)}, u32[]{:S(2)}) collective-permute-start(bf16[128,2048]{1,0:T(8,128)(2,1)S(1)} %constant_dynamic-update-slice_fusion.refs_0_), channel_id=1, source_target_pairs={{0,128},{8,40},{16,144},{24,56},{32,160},{40,8},{48,176},{56,24},{... | collective-permute-start | bytes 1572872 | tf_op jit(solution)/shard_map/ppermute | solution.py:339
  19.7 0.1 sub.59
  19.7 0.1 sub.63
  19.8 0.1 sub.66
  20.0 3.8 %copy.16.g_ref = bf16[128,64,64]{2,1,0:T(8,128)(2,1)} copy(bf16[128,64,64]{0,2,1:T(8,128)(2,1)S(1)} %copy-done.1) | data formatting | bytes 2097152 | tf_op args[6]
  23.8 0.7 copy.17.d_ref
  24.6 0.1 copy.14
  24.7 0.1 reshape.47
  24.8 0.1 copy.15
  24.9 0.1 reshape.48.lists
  25.0 3.7 %prepare.1.refs_8_ = bf16[32,272,256]{2,1,0:T(8,128)(2,1)} custom-call(bf16[128,64,64]{2,1,0:T(8,128)(2,1)} %copy.16.g_ref, bf16[128,64]{1,0:T(8,128)(2,1)} %copy.17.d_ref), custom_call_target="tpu_custom_call" | custom-call | tf_op jit(solution)/shard_map/prepare/pallas_call | solution.py:68
  28.7 0.5 collective-permute-start.7
  29.2 1.1 %collective-permute-done.4.refs_2_ = bf16[128,2048]{1,0:T(8,128)(2,1)S(1)} collective-permute-done((bf16[128,2048]{1,0:T(8,128)(2,1)S(1)}, bf16[128,2048]{1,0:T(8,128)(2,1)S(1)}, u32[]{:S(2)}, u32[]{:S(2)}) %collective-permute-start.4) | collective-permute-done | bytes 524320 | tf_op jit(solution)/shard_map/ppermute | solution.py:339
  30.3 1.4 %collective-permute-done.5.refs_3_ = bf16[128,2048]{1,0:T(8,128)(2,1)S(1)} collective-permute-done((bf16[128,2048]{1,0:T(8,128)(2,1)S(1)}, bf16[128,2048]{1,0:T(8,128)(2,1)S(1)}, u32[]{:S(2)}, u32[]{:S(2)}) %collective-permute-start.5) | collective-permute-done | bytes 524320 | tf_op jit(solution)/shard_map/ppermute | solution.py:339
  31.8 0.4 collective-permute-done.8.refs_6_
  32.2 1.4 %collective-permute-done.9.refs_7_ = bf16[128,2048]{1,0:T(8,128)(2,1)S(1)} collective-permute-done((bf16[128,2048]{1,0:T(8,128)(2,1)S(1)}, bf16[128,2048]{1,0:T(8,128)(2,1)S(1)}, u32[]{:S(2)}, u32[]{:S(2)}) %collective-permute-start.9) | collective-permute-done | bytes 524320 | tf_op jit(solution)/shard_map/ppermute | solution.py:340
  33.5 14.8 %revalue.1 = (f32[128,8,128]{2,1,0:T(8,128)S(1)}, f32[128,8,128]{2,1,0:T(8,128)S(1)}, f32[128,128]{1,0:T(8,128)S(1)}) custom-call(s32[32]{0:T(128)S(1)} %pad_add_fusion.slots, s32[8192]{0:T(1024)S(1)} %reshape.48.lists, s32[128]{0:T(128)S(1)} %copy-done, s32[128]{0:T(128)S(1)} %fusion.2.own, bf16[128,2048]{1,0:T(8,128)(2,1)S(1)} %constant_dynamic-update-slice_fusion.refs_0_, ...), custom_call_target="tpu_custom_call" | custom-call | tf_op jit(solution)/shard_map/revalue/pallas_call | solution.py:167
  48.3 0.2 collective-permute-start.10
  48.5 1.8 %collective-permute-done.10 = f32[128,8,128]{2,1,0:T(8,128)S(1)} collective-permute-done((f32[128,8,128]{2,1,0:T(8,128)S(1)}, f32[128,8,128]{2,1,0:T(8,128)S(1)}, u32[]{:S(2)}, u32[]{:S(2)}) %collective-permute-start.10) | collective-permute-done | bytes 524320 | tf_op jit(solution)/shard_map/ppermute | solution.py:356
  50.4 18.3 %all_to_all.10.p_ref = f32[16,64,128]{2,1,0:T(8,128)S(1)} all-to-all(f32[16,64,128]{2,1,0:T(8,128)S(1)} %bitcast.4), channel_id=1, replica_groups={{0,16,32,48,64,80,96,112,128,144,160,176,192,208,224,240},{8,24,40,56,7..., dimensions={0} | all-to-all | bytes 1048576 | tf_op jit(solution)/shard_map/all_to_all | solution.py:358
  68.7 0.3 moments.1
  69.0 15.6 %all_to_all.11.p_ref = f32[8,16,128]{2,1,0:T(8,128)S(1)} all-to-all(f32[8,16,128]{2,1,0:T(8,128)S(1)} %get-tuple-element.13), channel_id=1, replica_groups=mesh['set'=32,'path'=8] {'path'}, dimensions={0} | all-to-all | bytes 131072 | tf_op jit(solution)/shard_map/all_to_all | solution.py:362
  84.7 2.3 %expose.1 = f32[2,8,512]{2,1,0:T(8,128)} custom-call(f32[8,16,128]{2,1,0:T(8,128)S(1)} %all_to_all.11.p_ref, f32[64,128]{1,0:T(8,128)S(1)} %get-tuple-element.14.n_ref, f32[128,128]{1,0:T(8,128)S(1)} %get-tuple-element.12.b_ref), custom_call_target="tpu_custom_call" | custom-call | tf_op jit(solution)/shard_map/expose/pallas_call | solution.py:266
  (29 shorter events, 0.4 us)
Async XLA Ops:
  0.6 19.0 %copy-start.4 = (s32[4]{0:T(128)S(1)}, s32[4]{0:T(128)}, u32[]{:S(2)}) copy-start(s32[4]{0:T(128)} %constant.119.clone) | copy-start | bytes 52
  0.6 19.3 %copy-start.1 = (bf16[128,64,64]{0,2,1:T(8,128)(2,1)S(1)}, bf16[128,64,64]{0,2,1:T(8,128)(2,1)}, u32[]{:S(2)}) copy-start(bf16[128,64,64]{0,2,1:T(8,128)(2,1)} %param.16) | copy-start | bytes 3145732
  0.7 23.2 %copy-start.3 = (bf16[128,64]{0,1:T(8,128)(2,1)S(1)}, bf16[128,64]{0,1:T(8,128)(2,1)}, u32[]{:S(2)}) copy-start(bf16[128,64]{0,1:T(8,128)(2,1)} %param.15) | copy-start | bytes 49156
  0.7 23.9 %copy-start.2 = (s32[128,64]{0,1:T(8,128)S(1)}, s32[128,64]{0,1:T(8,128)}, u32[]{:S(2)}) copy-start(s32[128,64]{0,1:T(8,128)} %param.14) | copy-start | bytes 98308
  5.7 5.3 %collective-permute-start = (bf16[32,2048]{1,0:T(8,128)(2,1)S(1)}, bf16[32,2048]{1,0:T(8,128)(2,1)S(1)}, u32[]{:S(2)}, u32[]{:S(2)}) collective-permute-start(bf16[32,2048]{1,0:T(8,128)(2,1)S(1)} %get-tuple-element.9), channel_id=1, source_target_pairs={{0,16},{8,72},{16,32},{24,88},{32,48},{40,104},{48,0},{56,120},{64... | collective-permute-start | bytes 393224 | tf_op jit(solution)/shard_map/ppermute | solution.py:337
  7.3 5.0 %collective-permute-start.1 = (bf16[32,2048]{1,0:T(8,128)(2,1)S(1)}, bf16[32,2048]{1,0:T(8,128)(2,1)S(1)}, u32[]{:S(2)}, u32[]{:S(2)}) collective-permute-start(bf16[32,2048]{1,0:T(8,128)(2,1)S(1)} %get-tuple-element.9), channel_id=1, source_target_pairs={{0,48},{8,200},{16,0},{24,216},{32,16},{40,232},{48,32},{56,248},{... | collective-permute-start | bytes 393224 | tf_op jit(solution)/shard_map/ppermute | solution.py:337
  8.1 6.5 %collective-permute-start.2 = (bf16[32,2048]{1,0:T(8,128)(2,1)S(1)}, bf16[32,2048]{1,0:T(8,128)(2,1)S(1)}, u32[]{:S(2)}, u32[]{:S(2)}) collective-permute-start(bf16[32,2048]{1,0:T(8,128)(2,1)S(1)} %get-tuple-element.9), channel_id=1, source_target_pairs={{0,32},{8,136},{16,48},{24,152},{32,0},{40,168},{48,16},{56,184},{... | collective-permute-start | bytes 393224 | tf_op jit(solution)/shard_map/ppermute | solution.py:337
  14.6 14.1 %collective-permute-start.3 = (bf16[128,2048]{1,0:T(8,128)(2,1)S(1)}, bf16[128,2048]{1,0:T(8,128)(2,1)S(1)}, u32[]{:S(2)}, u32[]{:S(2)}) collective-permute-start(bf16[128,2048]{1,0:T(8,128)(2,1)S(1)} %constant_dynamic-update-slice_fusion.refs_0_), channel_id=1, source_target_pairs={{0,64},{8,24},{16,80},{24,40},{32,96},{40,56},{48,112},{56,8},{64,... | collective-permute-start | bytes 1572872 | tf_op jit(solution)/shard_map/ppermute | solution.py:339
  15.9 14.3 %collective-permute-start.4 = (bf16[128,2048]{1,0:T(8,128)(2,1)S(1)}, bf16[128,2048]{1,0:T(8,128)(2,1)S(1)}, u32[]{:S(2)}, u32[]{:S(2)}) collective-permute-start(bf16[128,2048]{1,0:T(8,128)(2,1)S(1)} %constant_dynamic-update-slice_fusion.refs_0_), channel_id=1, source_target_pairs={{0,192},{8,56},{16,208},{24,8},{32,224},{40,24},{48,240},{56,40},{... | collective-permute-start | bytes 1572872 | tf_op jit(solution)/shard_map/ppermute | solution.py:339
  17.9 13.7 %collective-permute-start.5 = (bf16[128,2048]{1,0:T(8,128)(2,1)S(1)}, bf16[128,2048]{1,0:T(8,128)(2,1)S(1)}, u32[]{:S(2)}, u32[]{:S(2)}) collective-permute-start(bf16[128,2048]{1,0:T(8,128)(2,1)S(1)} %constant_dynamic-update-slice_fusion.refs_0_), channel_id=1, source_target_pairs={{0,128},{8,40},{16,144},{24,56},{32,160},{40,8},{48,176},{56,24},{... | collective-permute-start | bytes 1572872 | tf_op jit(solution)/shard_map/ppermute | solution.py:339
  20.0 11.7 %copy-start.5 = (s32[128]{0:T(128)S(1)}, s32[128]{0:T(128)}, u32[]{:S(2)}) copy-start(s32[128]{0:T(128)} %param.18) | copy-start | bytes 1540
  20.0 13.5 %copy-start = (s32[128]{0:T(128)S(1)}, s32[128]{0:T(128)}, u32[]{:S(2)}) copy-start(s32[128]{0:T(128)} %cur.1) | copy-start | bytes 1540
  28.7 3.1 %collective-permute-start.6 = (bf16[128,2048]{1,0:T(8,128)(2,1)S(1)}, bf16[128,2048]{1,0:T(8,128)(2,1)S(1)}, u32[]{:S(2)}, u32[]{:S(2)}) collective-permute-start(bf16[128,2048]{1,0:T(8,128)(2,1)S(1)} %constant_dynamic-update-slice_fusion.refs_0_), channel_id=1, source_target_pairs={{0,8},{8,0},{16,24},{24,16},{32,40},{40,32},{48,56},{56,48},{64,72... | collective-permute-start | bytes 1572872 | tf_op jit(solution)/shard_map/ppermute | solution.py:340
  28.7 3.1 %collective-permute-start.7 = (bf16[128,2048]{1,0:T(8,128)(2,1)S(1)}, bf16[128,2048]{1,0:T(8,128)(2,1)S(1)}, u32[]{:S(2)}, u32[]{:S(2)}) collective-permute-start(bf16[128,2048]{1,0:T(8,128)(2,1)S(1)} %collective-permute-done.3.refs_1_), channel_id=1, source_target_pairs={{0,8},{8,0},{16,24},{24,16},{32,40},{40,32},{48,56},{56,48},{64,72... | collective-permute-start | bytes 1572872 | tf_op jit(solution)/shard_map/ppermute | solution.py:340
  30.3 1.9 %collective-permute-start.8 = (bf16[128,2048]{1,0:T(8,128)(2,1)S(1)}, bf16[128,2048]{1,0:T(8,128)(2,1)S(1)}, u32[]{:S(2)}, u32[]{:S(2)}) collective-permute-start(bf16[128,2048]{1,0:T(8,128)(2,1)S(1)} %collective-permute-done.4.refs_2_), channel_id=1, source_target_pairs={{0,8},{8,0},{16,24},{24,16},{32,40},{40,32},{48,56},{56,48},{64,72... | collective-permute-start | bytes 1572872 | tf_op jit(solution)/shard_map/ppermute | solution.py:340
  31.6 1.9 %collective-permute-start.9 = (bf16[128,2048]{1,0:T(8,128)(2,1)S(1)}, bf16[128,2048]{1,0:T(8,128)(2,1)S(1)}, u32[]{:S(2)}, u32[]{:S(2)}) collective-permute-start(bf16[128,2048]{1,0:T(8,128)(2,1)S(1)} %collective-permute-done.5.refs_3_), channel_id=1, source_target_pairs={{0,8},{8,0},{16,24},{24,16},{32,40},{40,32},{48,56},{56,48},{64,72... | collective-permute-start | bytes 1572872 | tf_op jit(solution)/shard_map/ppermute | solution.py:340
  48.3 2.0 %collective-permute-start.10 = (f32[128,8,128]{2,1,0:T(8,128)S(1)}, f32[128,8,128]{2,1,0:T(8,128)S(1)}, u32[]{:S(2)}, u32[]{:S(2)}) collective-permute-start(f32[128,8,128]{2,1,0:T(8,128)S(1)} %get-tuple-element.11), channel_id=1, source_target_pairs={{0,8},{8,0},{16,24},{24,16},{32,40},{40,32},{48,56},{56,48},{64,72... | collective-permute-start | bytes 1572872 | tf_op jit(solution)/shard_map/ppermute | solution.py:356

commit v3 on v2

--- a/solution.py
+++ b/solution.py
@@ -14,7 +14,7 @@
 ROWS = 16
 LANES = 128
 GRID = 4
-HOPS = (0, 1, 3, 2)
+HOPS = (0, 2, 1, 3)
 NG = 4
 PITCH = 9
 SUB = 8
@@ -78,7 +78,7 @@
     )(gamma, delta)
 
 
-def revalue(slots, lists, currency, owner, arrays, gd, sets, depth):
+def revalue(slots, lists, currency, owner, arrays, gd, end, sets, depth):
     factors = arrays[0].shape[1]
     blocks = arrays[0].shape[0] // (STEPS * ROWS)
     sources = len(arrays) * blocks
@@ -91,10 +91,12 @@
 
     def body(slots, lists, cur, own, *refs):
         arrs = refs[:len(arrays)]
-        gd_hbm, mine, theirs, base = refs[len(arrays):len(arrays) + 4]
-        sl, st, xa, xb, rates, gdv, net, gsem = refs[len(arrays) + 4:]
+        gd_hbm, end_ref, mine, theirs, base, end_hbm = refs[len(arrays):len(arrays) + 6]
+        sl, st, xa, xb, rates, gdv, net, gsem, esem = refs[len(arrays) + 6:]
         gcp = pltpu.make_async_copy(gd_hbm, gdv, gsem)
         gcp.start()
+        ecp = pltpu.make_async_copy(end_ref, end_hbm, esem)
+        ecp.start()
         net[...] = jnp.zeros(net.shape, F32)
         for a in range(len(arrays)):
             for e in range(blocks):
@@ -106,19 +108,19 @@
                 for q in range(chunks):
                     blk = sl[pl.ds(per_chunk * q, per_chunk), pl.ds(t * ROWS, ROWS), pl.ds(f0, tile)]
                     o = jnp.transpose(blk.reshape(LANES, tile).astype(F32))
-                    st[pl.ds(f0 * SUB + (t * chunks + q), tile, stride=SUB), :] = o
+                    st[pl.ds(f0 * PITCH + (t * chunks + q), tile, stride=PITCH), :] = o
             return carry
 
         lax.fori_loop(0, factors // tile, turn, 0)
         for c in range(NB):
-            b = st[pl.ds(c * SUB, SUB), :]
+            b = st[pl.ds(c * PITCH, SUB), :]
             base[pl.ds(c * SUB, SUB), :] = b
             rates[c] = jnp.exp(0.2 * b)
 
         def picks(j, x, k0, k1):
             for k in range(k0, k1):
                 i = lists.at[pl.ds(k * groups, groups)][j]
-                x[pl.ds(k * PITCH, SUB), :] = st[pl.ds(pl.multiple_of(i, SUB), SUB), :]
+                x[pl.ds(k * PITCH, SUB), :] = st[pl.ds(i, SUB), :]
 
         sub = lax.broadcasted_iota(jnp.int32, (SUB, LANES), 0)
         halves = SUB // 2
@@ -159,6 +161,7 @@
         half = counterparties // 2
         theirs[...] = net[pl.ds(half, half)]
         mine[...] = net[pl.ds(0, half)]
+        ecp.wait()
 
     smem = pl.BlockSpec(memory_space=pltpu.SMEM)
     hbm = pl.BlockSpec(memory_space=pltpu.HBM)
@@ -166,17 +169,20 @@
     half_shape = pltpu.VMEM((counterparties // 2, SUB, LANES), F32)
     return pl.pallas_call(
         body,
-        in_specs=[smem] * 4 + [vmem] * len(arrays) + [hbm],
-        out_specs=(vmem, vmem, vmem),
-        out_shape=(half_shape, half_shape, pltpu.VMEM((NB * SUB, LANES), F32)),
+        in_specs=[smem] * 4 + [vmem] * len(arrays) + [hbm, vmem],
+        out_specs=(vmem, vmem, vmem, hbm),
+        out_shape=(
+            half_shape, half_shape, pltpu.VMEM((NB * SUB, LANES), F32), jax.ShapeDtypeStruct(end.shape, F32),
+        ),
         scratch_shapes=[
             pltpu.VMEM((sources, STEPS * ROWS, factors), BF16),
-            pltpu.VMEM((factors * SUB, LANES), F32),
+            pltpu.VMEM((factors * PITCH, LANES), F32),
             pltpu.VMEM((wide * PITCH, LANES), F32),
             pltpu.VMEM((wide * PITCH, LANES), F32),
             pltpu.VMEM((NB, SUB, LANES), F32),
             pltpu.VMEM(gd.shape, BF16),
             pltpu.VMEM((counterparties, SUB, LANES), F32),
+            pltpu.SemaphoreType.DMA(()),
             pltpu.SemaphoreType.DMA(()),
         ],
         compiler_params=pltpu.CompilerParams(vmem_limit_bytes=40 * 1024 * 1024),
@@ -185,6 +191,7 @@
         slots, lists, currency, owner,
         *[on_chip(a) for a in arrays],
         pltpu.with_memory_space_constraint(gd, pltpu.HBM),
+        on_chip(end),
     )
 
 
@@ -235,7 +242,7 @@
 def expose(payload, net, base, total):
     chunks = SUB // STEPS
 
-    def body(p_ref, n_ref, b_ref, o_ref):
+    def body(p_ref, n_ref, b_ref, o_hbm, o_ref, sem):
         acc = jnp.sum(p_ref[...], axis=0) * (1.0 / total)
         row = lax.broadcasted_iota(jnp.int32, (NBP + SUB, LANES), 0)
         lane = lax.broadcasted_iota(jnp.int32, (NBP + SUB, LANES), 1)
@@ -257,17 +264,23 @@
                 sys[t] = jnp.where(lane == k, c, a - c * r)
         for t in range(STEPS):
             coef = sys[t][NBP:, 0:NBP]
-            for q in range(chunks):
-                s = t * chunks + q
-                fitted = jnp.dot(coef, basis_rows(b_ref, s), precision=HIGH, preferred_element_type=F32)
-                n = n_ref[pl.ds(s, SUB, stride=SUB), :]
-                o_ref[t, :, q * LANES:(q + 1) * LANES] = jnp.maximum(n - 0.9 * fitted, 0.0)
+            steps = [t * chunks + q for q in range(chunks)]
+            fitted = jnp.dot(
+                coef, jnp.concatenate([basis_rows(b_ref, s) for s in steps], axis=1),
+                precision=HIGH, preferred_element_type=F32,
+            )
+            n = jnp.concatenate([n_ref[pl.ds(s, SUB, stride=SUB), :] for s in steps], axis=1)
+            o_ref[t] = jnp.maximum(n - 0.9 * fitted, 0.0)
+        cp = pltpu.make_async_copy(o_ref, o_hbm, sem)
+        cp.start()
+        cp.wait()
 
     return pl.pallas_call(
         body,
         in_specs=[VMEM_SPEC] * 3,
-        out_specs=VMEM_SPEC,
+        out_specs=pl.BlockSpec(memory_space=pltpu.HBM),
         out_shape=jax.ShapeDtypeStruct((STEPS, SUB, chunks * LANES), F32),
+        scratch_shapes=[pltpu.VMEM((STEPS, SUB, chunks * LANES), F32), pltpu.SemaphoreType.DMA(())],
         name="expose",
     )(on_chip(payload), on_chip(net), on_chip(base))
 
@@ -312,7 +325,7 @@
         out_specs=(vmem, vmem),
         out_shape=(
             pltpu.VMEM((STEPS * rows, factors), BF16),
-            jax.ShapeDtypeStruct((rows, factors), F32),
+            pltpu.VMEM((rows, factors), F32),
         ),
         scratch_shapes=[
             pltpu.VMEM((STEPS * rows, factors), BF16),
@@ -348,11 +361,13 @@
         return (((py - dy) % GRID * GRID + (px - dx) % GRID) * 2 + c).reshape(-1)
 
     slots = jnp.concatenate([slots_of(core), slots_of(1 - core)]).astype(jnp.int32)
-    lists = (factor_lists * SUB).reshape(sets // NG, NG * depth).T.reshape(-1)
+    lists = (factor_lists * PITCH).reshape(sets // NG, NG * depth).T.reshape(-1)
     place = jnp.where((owner // SUB) % 2 == core, 0, 128) + owner // (2 * SUB) * SUB + owner % SUB
 
     gd = prepare(gamma, delta)
-    mine, theirs, base = revalue(slots, lists, currency, place, plane + other, gd, sets, depth)
+    mine, theirs, base, state = revalue(
+        slots, lists, currency, place, plane + other, gd, state, sets, depth
+    )
     mine = mine + lax.ppermute(theirs, "set", core_pairs())
     chips = [[i * 2 + c for i in range(GRID * GRID)] for c in range(2)]
     parts = lax.all_to_all(

time: 87.2 us -> 86.9 us (level)
  waiting for transfers between devices: 10.5 us -> 9.29 us
  starting transfers between devices: 10.1 us -> 11.3 us
    ppermute x3, waiting for transfers between devices: 2.44 us -> 0.98 us  [per_device(): lax.ppermute(line, 'set', hop_pairs(h, 1))]
    all_to_all x1, blocking collectives: 15.6 us -> 16.7 us  [per_device(): payload = lax.all_to_all(payload, 'path', 0, 0)]
where the time goes in v3:
time: 86.9 us; the launch traced here: 86.7 us
  blocking collectives  34.3 us (39%)
  Pallas kernels  25.4 us (29%)
  starting transfers between devices  11.3 us (13%)
  waiting for transfers between devices  9.29 us (11%)
  local copies, waits for them, and re-layouts  5.32 us (6%)
    all_to_all x1, blocking collectives, per_device(): lax.all_to_all(mine.reshape(GRID * GRID, SUB * SUB, LANES), 'set', 0, 0,...  17.7 us
    all_to_all x1, blocking collectives, per_device(): payload = lax.all_to_all(payload, 'path', 0, 0)  16.7 us
    pallas_call x1, Pallas kernels, revalue(): pl.pallas_call(body, in_specs=[smem] * 4 + [vmem] * len(arrays) + [hbm, v...  14.8 us
    ppermute x3, starting transfers between devices, per_device(): lax.ppermute(line, 'set', hop_pairs(h, 1))  5.83 us
    unnamed x17, local copies, waits for them, and re-layouts  4.61 us
    ppermute x3, waiting for transfers between devices, per_device(): lax.ppermute(slab, 'set', hop_pairs(h, 0))  4.48 us
    pallas_call x1, Pallas kernels, evolve(): pl.pallas_call(body, in_specs=[hbm] * 4, out_specs=(vmem, vmem), out_shap...  4.36 us
    ppermute x3, starting transfers between devices, per_device(): lax.ppermute(slab, 'set', hop_pairs(h, 0))  4.24 us
  transfers between devices with their start and end apart: 11, of which 8 were waited for; matrix products, arithmetic and copies ran while one was open for 6% of the time, Pallas kernels for 4%

profile of v3, /device:TPU:2, one launch (start us, length us, event | category | flops | bytes accessed | tf_op | source)
XLA Modules:
  0.0 86.7 jit_solution(147729346039891404)
XLA Ops:
  0.7 4.4 %evolve.1 = (bf16[32,2048]{1,0:T(8,128)(2,1)S(1)}, f32[16,2048]{1,0:T(8,128)S(1)}) custom-call(bf16[32,2048]{1,0:T(8,128)(2,1)} %bitcast.5, bf16[2048,2048]{1,0:T(8,128)(2,1)} %l_hbm.1, f32[16,2048]{1,0:T(8,128)} %s_hbm.1, f32[1,2048]{1,0:T(1,128)} %bitcast.7), custom_call_target="tpu_custom_call" | custom-call | tf_op jit(solution)/shard_map/evolve/pallas_call | solution.py:322
  5.0 2.2 %collective-permute-start = (bf16[32,2048]{1,0:T(8,128)(2,1)S(1)}, bf16[32,2048]{1,0:T(8,128)(2,1)S(1)}, u32[]{:S(2)}, u32[]{:S(2)}) collective-permute-start(bf16[32,2048]{1,0:T(8,128)(2,1)S(1)} %get-tuple-element.10), channel_id=1, source_target_pairs={{0,32},{8,136},{16,48},{24,152},{32,0},{40,168},{48,16},{56,184},{... | collective-permute-start | bytes 393224 | tf_op jit(solution)/shard_map/ppermute | solution.py:350
  7.3 1.6 %collective-permute-start.1 = (bf16[32,2048]{1,0:T(8,128)(2,1)S(1)}, bf16[32,2048]{1,0:T(8,128)(2,1)S(1)}, u32[]{:S(2)}, u32[]{:S(2)}) collective-permute-start(bf16[32,2048]{1,0:T(8,128)(2,1)S(1)} %get-tuple-element.10), channel_id=1, source_target_pairs={{0,16},{8,72},{16,32},{24,88},{32,48},{40,104},{48,0},{56,120},{64... | collective-permute-start | bytes 393224 | tf_op jit(solution)/shard_map/ppermute | solution.py:350
  8.8 0.4 collective-permute-start.2
  9.3 2.3 %collective-permute-done = bf16[32,2048]{1,0:T(8,128)(2,1)S(1)} collective-permute-done((bf16[32,2048]{1,0:T(8,128)(2,1)S(1)}, bf16[32,2048]{1,0:T(8,128)(2,1)S(1)}, u32[]{:S(2)}, u32[]{:S(2)}) %collective-permute-start) | collective-permute-done | bytes 131104 | tf_op jit(solution)/shard_map/ppermute | solution.py:350
  11.6 1.4 %collective-permute-done.1 = bf16[32,2048]{1,0:T(8,128)(2,1)S(1)} collective-permute-done((bf16[32,2048]{1,0:T(8,128)(2,1)S(1)}, bf16[32,2048]{1,0:T(8,128)(2,1)S(1)}, u32[]{:S(2)}, u32[]{:S(2)}) %collective-permute-start.1) | collective-permute-done | bytes 131104 | tf_op jit(solution)/shard_map/ppermute | solution.py:350
  13.1 0.8 collective-permute-done.2
  13.8 2.6 %collective-permute-start.3 = (bf16[128,2048]{1,0:T(8,128)(2,1)S(1)}, bf16[128,2048]{1,0:T(8,128)(2,1)S(1)}, u32[]{:S(2)}, u32[]{:S(2)}) collective-permute-start(bf16[128,2048]{1,0:T(8,128)(2,1)S(1)} %constant_dynamic-update-slice_fusion.refs_0_), channel_id=1, source_target_pairs={{0,128},{8,40},{16,144},{24,56},{32,160},{40,8},{48,176},{56,24},{... | collective-permute-start | bytes 1572872 | tf_op jit(solution)/shard_map/ppermute | solution.py:352
  16.4 0.7 collective-permute-start.4
  17.1 2.6 %collective-permute-start.5 = (bf16[128,2048]{1,0:T(8,128)(2,1)S(1)}, bf16[128,2048]{1,0:T(8,128)(2,1)S(1)}, u32[]{:S(2)}, u32[]{:S(2)}) collective-permute-start(bf16[128,2048]{1,0:T(8,128)(2,1)S(1)} %constant_dynamic-update-slice_fusion.refs_0_), channel_id=1, source_target_pairs={{0,192},{8,56},{16,208},{24,8},{32,224},{40,24},{48,240},{56,40},{... | collective-permute-start | bytes 1572872 | tf_op jit(solution)/shard_map/ppermute | solution.py:352
  19.7 0.1 sub.59
  19.8 0.1 sub.63
  20.1 3.8 %copy.16.g_ref = bf16[128,64,64]{2,1,0:T(8,128)(2,1)} copy(bf16[128,64,64]{0,2,1:T(8,128)(2,1)S(1)} %copy-done.1) | data formatting | bytes 2097152 | tf_op args[6]
  23.9 0.7 copy.17.d_ref
  24.6 0.1 copy.14
  24.7 0.1 reshape.47
  24.8 0.1 copy.15
  24.9 0.1 reshape.48.lists
  25.0 3.7 %prepare.1.refs_8_ = bf16[32,272,256]{2,1,0:T(8,128)(2,1)} custom-call(bf16[128,64,64]{2,1,0:T(8,128)(2,1)} %copy.16.g_ref, bf16[128,64]{1,0:T(8,128)(2,1)} %copy.17.d_ref), custom_call_target="tpu_custom_call" | custom-call | tf_op jit(solution)/shard_map/prepare/pallas_call | solution.py:68
  28.7 0.5 collective-permute-start.7
  29.2 1.0 %collective-permute-done.4.refs_2_ = bf16[128,2048]{1,0:T(8,128)(2,1)S(1)} collective-permute-done((bf16[128,2048]{1,0:T(8,128)(2,1)S(1)}, bf16[128,2048]{1,0:T(8,128)(2,1)S(1)}, u32[]{:S(2)}, u32[]{:S(2)}) %collective-permute-start.4) | collective-permute-done | bytes 524320 | tf_op jit(solution)/shard_map/ppermute | solution.py:352
  30.2 0.5 collective-permute-start.9
  30.9 0.5 collective-permute-done.7.refs_5_
  31.4 0.7 collective-permute-done.8.refs_6_
  32.1 0.7 collective-permute-done.9.refs_7_
  32.9 14.8 %revalue.1 = (f32[128,8,128]{2,1,0:T(8,128)S(1)}, f32[128,8,128]{2,1,0:T(8,128)S(1)}, f32[128,128]{1,0:T(8,128)S(1)}, f32[16,2048]{1,0:T(8,128)}) custom-call(s32[32]{0:T(128)S(1)} %pad_add_fusion.slots, s32[8192]{0:T(1024)S(1)} %reshape.48.lists, s32[128]{0:T(128)S(1)} %copy-done, s32[128]{0:T(128)S(1)} %fusion.2.own, ...), custom_call_target="tpu_custom_call" | custom-call | tf_op jit(solution)/shard_map/revalue/pallas_call | solution.py:170
  47.7 0.2 collective-permute-start.10
  47.9 1.8 %collective-permute-done.10 = f32[128,8,128]{2,1,0:T(8,128)S(1)} collective-permute-done((f32[128,8,128]{2,1,0:T(8,128)S(1)}, f32[128,8,128]{2,1,0:T(8,128)S(1)}, u32[]{:S(2)}, u32[]{:S(2)}) %collective-permute-start.10) | collective-permute-done | bytes 524320 | tf_op jit(solution)/shard_map/ppermute | solution.py:371
  49.8 17.7 %all_to_all.10.p_ref = f32[16,64,128]{2,1,0:T(8,128)S(1)} all-to-all(f32[16,64,128]{2,1,0:T(8,128)S(1)} %bitcast.4), channel_id=1, replica_groups={{0,16,32,48,64,80,96,112,128,144,160,176,192,208,224,240},{8,24,40,56,7..., dimensions={0} | all-to-all | bytes 1048576 | tf_op jit(solution)/shard_map/all_to_all | solution.py:373
  67.5 0.3 moments.1
  67.8 16.7 %all_to_all.11.p_ref = f32[8,16,128]{2,1,0:T(8,128)S(1)} all-to-all(f32[8,16,128]{2,1,0:T(8,128)S(1)} %get-tuple-element.15), channel_id=1, replica_groups=mesh['set'=32,'path'=8] {'path'}, dimensions={0} | all-to-all | bytes 131072 | tf_op jit(solution)/shard_map/all_to_all | solution.py:377
  84.5 2.2 %expose.1 = f32[2,8,512]{2,1,0:T(8,128)} custom-call(f32[8,16,128]{2,1,0:T(8,128)S(1)} %all_to_all.11.p_ref, f32[64,128]{1,0:T(8,128)S(1)} %get-tuple-element.16.n_ref, f32[128,128]{1,0:T(8,128)S(1)} %get-tuple-element.14.b_ref), custom_call_target="tpu_custom_call" | custom-call | tf_op jit(solution)/shard_map/expose/pallas_call | solution.py:278
  (29 shorter events, 0.5 us)
Async XLA Ops:
  0.6 19.0 %copy-start.4 = (s32[4]{0:T(128)S(1)}, s32[4]{0:T(128)}, u32[]{:S(2)}) copy-start(s32[4]{0:T(128)} %constant.120.clone) | copy-start | bytes 52
  0.6 19.4 %copy-start.1 = (bf16[128,64,64]{0,2,1:T(8,128)(2,1)S(1)}, bf16[128,64,64]{0,2,1:T(8,128)(2,1)}, u32[]{:S(2)}) copy-start(bf16[128,64,64]{0,2,1:T(8,128)(2,1)} %param.16) | copy-start | bytes 3145732
  0.7 23.2 %copy-start.3 = (bf16[128,64]{0,1:T(8,128)(2,1)S(1)}, bf16[128,64]{0,1:T(8,128)(2,1)}, u32[]{:S(2)}) copy-start(bf16[128,64]{0,1:T(8,128)(2,1)} %param.15) | copy-start | bytes 49156
  0.7 24.0 %copy-start.2 = (s32[128,64]{0,1:T(8,128)S(1)}, s32[128,64]{0,1:T(8,128)}, u32[]{:S(2)}) copy-start(s32[128,64]{0,1:T(8,128)} %param.14) | copy-start | bytes 98308
  5.0 6.6 %collective-permute-start = (bf16[32,2048]{1,0:T(8,128)(2,1)S(1)}, bf16[32,2048]{1,0:T(8,128)(2,1)S(1)}, u32[]{:S(2)}, u32[]{:S(2)}) collective-permute-start(bf16[32,2048]{1,0:T(8,128)(2,1)S(1)} %get-tuple-element.10), channel_id=1, source_target_pairs={{0,32},{8,136},{16,48},{24,152},{32,0},{40,168},{48,16},{56,184},{... | collective-permute-start | bytes 393224 | tf_op jit(solution)/shard_map/ppermute | solution.py:350
  7.3 5.8 %collective-permute-start.1 = (bf16[32,2048]{1,0:T(8,128)(2,1)S(1)}, bf16[32,2048]{1,0:T(8,128)(2,1)S(1)}, u32[]{:S(2)}, u32[]{:S(2)}) collective-permute-start(bf16[32,2048]{1,0:T(8,128)(2,1)S(1)} %get-tuple-element.10), channel_id=1, source_target_pairs={{0,16},{8,72},{16,32},{24,88},{32,48},{40,104},{48,0},{56,120},{64... | collective-permute-start | bytes 393224 | tf_op jit(solution)/shard_map/ppermute | solution.py:350
  8.8 5.0 %collective-permute-start.2 = (bf16[32,2048]{1,0:T(8,128)(2,1)S(1)}, bf16[32,2048]{1,0:T(8,128)(2,1)S(1)}, u32[]{:S(2)}, u32[]{:S(2)}) collective-permute-start(bf16[32,2048]{1,0:T(8,128)(2,1)S(1)} %get-tuple-element.10), channel_id=1, source_target_pairs={{0,48},{8,200},{16,0},{24,216},{32,16},{40,232},{48,32},{56,248},{... | collective-permute-start | bytes 393224 | tf_op jit(solution)/shard_map/ppermute | solution.py:350
  13.8 14.9 %collective-permute-start.3 = (bf16[128,2048]{1,0:T(8,128)(2,1)S(1)}, bf16[128,2048]{1,0:T(8,128)(2,1)S(1)}, u32[]{:S(2)}, u32[]{:S(2)}) collective-permute-start(bf16[128,2048]{1,0:T(8,128)(2,1)S(1)} %constant_dynamic-update-slice_fusion.refs_0_), channel_id=1, source_target_pairs={{0,128},{8,40},{16,144},{24,56},{32,160},{40,8},{48,176},{56,24},{... | collective-permute-start | bytes 1572872 | tf_op jit(solution)/shard_map/ppermute | solution.py:352
  16.4 13.8 %collective-permute-start.4 = (bf16[128,2048]{1,0:T(8,128)(2,1)S(1)}, bf16[128,2048]{1,0:T(8,128)(2,1)S(1)}, u32[]{:S(2)}, u32[]{:S(2)}) collective-permute-start(bf16[128,2048]{1,0:T(8,128)(2,1)S(1)} %constant_dynamic-update-slice_fusion.refs_0_), channel_id=1, source_target_pairs={{0,64},{8,24},{16,80},{24,40},{32,96},{40,56},{48,112},{56,8},{64,... | collective-permute-start | bytes 1572872 | tf_op jit(solution)/shard_map/ppermute | solution.py:352
  17.1 13.1 %collective-permute-start.5 = (bf16[128,2048]{1,0:T(8,128)(2,1)S(1)}, bf16[128,2048]{1,0:T(8,128)(2,1)S(1)}, u32[]{:S(2)}, u32[]{:S(2)}) collective-permute-start(bf16[128,2048]{1,0:T(8,128)(2,1)S(1)} %constant_dynamic-update-slice_fusion.refs_0_), channel_id=1, source_target_pairs={{0,192},{8,56},{16,208},{24,8},{32,224},{40,24},{48,240},{56,40},{... | collective-permute-start | bytes 1572872 | tf_op jit(solution)/shard_map/ppermute | solution.py:352
  20.1 10.8 %copy-start.5 = (s32[128]{0:T(128)S(1)}, s32[128]{0:T(128)}, u32[]{:S(2)}) copy-start(s32[128]{0:T(128)} %param.18) | copy-start | bytes 1540
  20.1 12.8 %copy-start = (s32[128]{0:T(128)S(1)}, s32[128]{0:T(128)}, u32[]{:S(2)}) copy-start(s32[128]{0:T(128)} %cur.1) | copy-start | bytes 1540
  28.7 2.1 %collective-permute-start.6 = (bf16[128,2048]{1,0:T(8,128)(2,1)S(1)}, bf16[128,2048]{1,0:T(8,128)(2,1)S(1)}, u32[]{:S(2)}, u32[]{:S(2)}) collective-permute-start(bf16[128,2048]{1,0:T(8,128)(2,1)S(1)} %constant_dynamic-update-slice_fusion.refs_0_), channel_id=1, source_target_pairs={{0,8},{8,0},{16,24},{24,16},{32,40},{40,32},{48,56},{56,48},{64,72... | collective-permute-start | bytes 1572872 | tf_op jit(solution)/shard_map/ppermute | solution.py:353
  28.7 2.7 %collective-permute-start.7 = (bf16[128,2048]{1,0:T(8,128)(2,1)S(1)}, bf16[128,2048]{1,0:T(8,128)(2,1)S(1)}, u32[]{:S(2)}, u32[]{:S(2)}) collective-permute-start(bf16[128,2048]{1,0:T(8,128)(2,1)S(1)} %collective-permute-done.3.refs_1_), channel_id=1, source_target_pairs={{0,8},{8,0},{16,24},{24,16},{32,40},{40,32},{48,56},{56,48},{64,72... | collective-permute-start | bytes 1572872 | tf_op jit(solution)/shard_map/ppermute | solution.py:353
  30.2 1.9 %collective-permute-start.8 = (bf16[128,2048]{1,0:T(8,128)(2,1)S(1)}, bf16[128,2048]{1,0:T(8,128)(2,1)S(1)}, u32[]{:S(2)}, u32[]{:S(2)}) collective-permute-start(bf16[128,2048]{1,0:T(8,128)(2,1)S(1)} %collective-permute-done.4.refs_2_), channel_id=1, source_target_pairs={{0,8},{8,0},{16,24},{24,16},{32,40},{40,32},{48,56},{56,48},{64,72... | collective-permute-start | bytes 1572872 | tf_op jit(solution)/shard_map/ppermute | solution.py:353
  30.2 2.7 %collective-permute-start.9 = (bf16[128,2048]{1,0:T(8,128)(2,1)S(1)}, bf16[128,2048]{1,0:T(8,128)(2,1)S(1)}, u32[]{:S(2)}, u32[]{:S(2)}) collective-permute-start(bf16[128,2048]{1,0:T(8,128)(2,1)S(1)} %collective-permute-done.5.refs_3_), channel_id=1, source_target_pairs={{0,8},{8,0},{16,24},{24,16},{32,40},{40,32},{48,56},{56,48},{64,72... | collective-permute-start | bytes 1572872 | tf_op jit(solution)/shard_map/ppermute | solution.py:353
  47.7 2.0 %collective-permute-start.10 = (f32[128,8,128]{2,1,0:T(8,128)S(1)}, f32[128,8,128]{2,1,0:T(8,128)S(1)}, u32[]{:S(2)}, u32[]{:S(2)}) collective-permute-start(f32[128,8,128]{2,1,0:T(8,128)S(1)} %get-tuple-element.13), channel_id=1, source_target_pairs={{0,8},{8,0},{16,24},{24,16},{32,40},{40,32},{48,56},{56,48},{64,72... | collective-permute-start | bytes 1572872 | tf_op jit(solution)/shard_map/ppermute | solution.py:371

commit v4 on v3

--- a/solution.py
+++ b/solution.py
@@ -14,7 +14,7 @@
 ROWS = 16
 LANES = 128
 GRID = 4
-HOPS = (0, 2, 1, 3)
+HOPS = (0, 2, 3, 1)
 NG = 4
 PITCH = 9
 SUB = 8

time: 86.9 us -> 86 us (0.990)
  blocking collectives: 34.3 us -> 33.2 us
    all_to_all x1, blocking collectives: 17.7 us -> 16.6 us  [per_device(): lax.all_to_all(mine.reshape(GRID * GRID, SUB * SUB, LANES), 'set', 0, 0,...]
    ppermute x3, waiting for transfers between devices: 0.98 us -> 1.89 us  [per_device(): lax.ppermute(line, 'set', hop_pairs(h, 1))]
  transfers between devices with their start and end apart: 11 -> 11, of which waited for: 8 -> 7; matrix products, arithmetic and copies ran while one was open for 6% -> 6% of each run, Pallas kernels for 4% -> 4%
where the time goes in v4:
time: 86 us; the launch traced here: 85.8 us
  blocking collectives  33.2 us (39%)
  Pallas kernels  25.4 us (30%)
  starting transfers between devices  10.8 us (13%)
  waiting for transfers between devices  9.99 us (12%)
  local copies, waits for them, and re-layouts  5.32 us (6%)
    all_to_all x1, blocking collectives, per_device(): payload = lax.all_to_all(payload, 'path', 0, 0)  16.6 us
    all_to_all x1, blocking collectives, per_device(): lax.all_to_all(mine.reshape(GRID * GRID, SUB * SUB, LANES), 'set', 0, 0,...  16.6 us
    pallas_call x1, Pallas kernels, revalue(): pl.pallas_call(body, in_specs=[smem] * 4 + [vmem] * len(arrays) + [hbm, v...  14.8 us
    ppermute x3, starting transfers between devices, per_device(): lax.ppermute(line, 'set', hop_pairs(h, 1))  5.31 us
    unnamed x17, local copies, waits for them, and re-layouts  4.61 us
    pallas_call x1, Pallas kernels, evolve(): pl.pallas_call(body, in_specs=[hbm] * 4, out_specs=(vmem, vmem), out_shap...  4.36 us
    ppermute x3, waiting for transfers between devices, per_device(): lax.ppermute(slab, 'set', hop_pairs(h, 0))  4.34 us
    ppermute x3, starting transfers between devices, per_device(): lax.ppermute(slab, 'set', hop_pairs(h, 0))  4.24 us
  transfers between devices with their start and end apart: 11, of which 7 were waited for; matrix products, arithmetic and copies ran while one was open for 6% of the time, Pallas kernels for 4%

profile of v4, /device:TPU:2, one launch (start us, length us, event | category | flops | bytes accessed | tf_op | source)
XLA Modules:
  0.0 85.8 jit_solution(5253382535913289426)
XLA Ops:
  0.7 4.4 %evolve.1 = (bf16[32,2048]{1,0:T(8,128)(2,1)S(1)}, f32[16,2048]{1,0:T(8,128)S(1)}) custom-call(bf16[32,2048]{1,0:T(8,128)(2,1)} %bitcast.5, bf16[2048,2048]{1,0:T(8,128)(2,1)} %l_hbm.1, f32[16,2048]{1,0:T(8,128)} %s_hbm.1, f32[1,2048]{1,0:T(1,128)} %bitcast.7), custom_call_target="tpu_custom_call" | custom-call | tf_op jit(solution)/shard_map/evolve/pallas_call | solution.py:322
  5.0 2.2 %collective-permute-start = (bf16[32,2048]{1,0:T(8,128)(2,1)S(1)}, bf16[32,2048]{1,0:T(8,128)(2,1)S(1)}, u32[]{:S(2)}, u32[]{:S(2)}) collective-permute-start(bf16[32,2048]{1,0:T(8,128)(2,1)S(1)} %get-tuple-element.10), channel_id=1, source_target_pairs={{0,32},{8,136},{16,48},{24,152},{32,0},{40,168},{48,16},{56,184},{... | collective-permute-start | bytes 393224 | tf_op jit(solution)/shard_map/ppermute | solution.py:350
  7.3 1.4 %collective-permute-start.1 = (bf16[32,2048]{1,0:T(8,128)(2,1)S(1)}, bf16[32,2048]{1,0:T(8,128)(2,1)S(1)}, u32[]{:S(2)}, u32[]{:S(2)}) collective-permute-start(bf16[32,2048]{1,0:T(8,128)(2,1)S(1)} %get-tuple-element.10), channel_id=1, source_target_pairs={{0,48},{8,200},{16,0},{24,216},{32,16},{40,232},{48,32},{56,248},{... | collective-permute-start | bytes 393224 | tf_op jit(solution)/shard_map/ppermute | solution.py:350
  8.7 0.6 collective-permute-start.2
  9.3 2.4 %collective-permute-done = bf16[32,2048]{1,0:T(8,128)(2,1)S(1)} collective-permute-done((bf16[32,2048]{1,0:T(8,128)(2,1)S(1)}, bf16[32,2048]{1,0:T(8,128)(2,1)S(1)}, u32[]{:S(2)}, u32[]{:S(2)}) %collective-permute-start) | collective-permute-done | bytes 131104 | tf_op jit(solution)/shard_map/ppermute | solution.py:350
  11.7 1.3 %collective-permute-done.1 = bf16[32,2048]{1,0:T(8,128)(2,1)S(1)} collective-permute-done((bf16[32,2048]{1,0:T(8,128)(2,1)S(1)}, bf16[32,2048]{1,0:T(8,128)(2,1)S(1)}, u32[]{:S(2)}, u32[]{:S(2)}) %collective-permute-start.1) | collective-permute-done | bytes 131104 | tf_op jit(solution)/shard_map/ppermute | solution.py:350
  13.0 0.6 collective-permute-done.2
  13.7 3.3 %collective-permute-start.3 = (bf16[128,2048]{1,0:T(8,128)(2,1)S(1)}, bf16[128,2048]{1,0:T(8,128)(2,1)S(1)}, u32[]{:S(2)}, u32[]{:S(2)}) collective-permute-start(bf16[128,2048]{1,0:T(8,128)(2,1)S(1)} %constant_dynamic-update-slice_fusion.refs_0_), channel_id=1, source_target_pairs={{0,128},{8,40},{16,144},{24,56},{32,160},{40,8},{48,176},{56,24},{... | collective-permute-start | bytes 1572872 | tf_op jit(solution)/shard_map/ppermute | solution.py:352
  17.0 1.1 %collective-permute-start.4 = (bf16[128,2048]{1,0:T(8,128)(2,1)S(1)}, bf16[128,2048]{1,0:T(8,128)(2,1)S(1)}, u32[]{:S(2)}, u32[]{:S(2)}) collective-permute-start(bf16[128,2048]{1,0:T(8,128)(2,1)S(1)} %constant_dynamic-update-slice_fusion.refs_0_), channel_id=1, source_target_pairs={{0,192},{8,56},{16,208},{24,8},{32,224},{40,24},{48,240},{56,40},{... | collective-permute-start | bytes 1572872 | tf_op jit(solution)/shard_map/ppermute | solution.py:352
  18.0 1.0 %collective-permute-start.5 = (bf16[128,2048]{1,0:T(8,128)(2,1)S(1)}, bf16[128,2048]{1,0:T(8,128)(2,1)S(1)}, u32[]{:S(2)}, u32[]{:S(2)}) collective-permute-start(bf16[128,2048]{1,0:T(8,128)(2,1)S(1)} %constant_dynamic-update-slice_fusion.refs_0_), channel_id=1, source_target_pairs={{0,64},{8,24},{16,80},{24,40},{32,96},{40,56},{48,112},{56,8},{64,... | collective-permute-start | bytes 1572872 | tf_op jit(solution)/shard_map/ppermute | solution.py:352
  19.1 0.1 sub.59
  19.1 0.1 sub.63
  19.2 0.1 sub.66
  19.4 3.8 %copy.16.g_ref = bf16[128,64,64]{2,1,0:T(8,128)(2,1)} copy(bf16[128,64,64]{0,2,1:T(8,128)(2,1)S(1)} %copy-done.1) | data formatting | bytes 2097152 | tf_op args[6]
  23.2 0.7 copy.17.d_ref
  24.0 0.1 copy.14
  24.1 0.1 reshape.47
  24.1 0.1 copy.15
  24.2 0.1 reshape.48.lists
  24.4 3.7 %prepare.1.refs_8_ = bf16[32,272,256]{2,1,0:T(8,128)(2,1)} custom-call(bf16[128,64,64]{2,1,0:T(8,128)(2,1)} %copy.16.g_ref, bf16[128,64]{1,0:T(8,128)(2,1)} %copy.17.d_ref), custom_call_target="tpu_custom_call" | custom-call | tf_op jit(solution)/shard_map/prepare/pallas_call | solution.py:68
  28.1 0.5 collective-permute-start.7
  28.6 1.9 %collective-permute-done.4.refs_2_ = bf16[128,2048]{1,0:T(8,128)(2,1)S(1)} collective-permute-done((bf16[128,2048]{1,0:T(8,128)(2,1)S(1)}, bf16[128,2048]{1,0:T(8,128)(2,1)S(1)}, u32[]{:S(2)}, u32[]{:S(2)}) %collective-permute-start.4) | collective-permute-done | bytes 524320 | tf_op jit(solution)/shard_map/ppermute | solution.py:352
  30.5 0.5 collective-permute-start.9
  31.1 1.3 %collective-permute-done.8.refs_6_ = bf16[128,2048]{1,0:T(8,128)(2,1)S(1)} collective-permute-done((bf16[128,2048]{1,0:T(8,128)(2,1)S(1)}, bf16[128,2048]{1,0:T(8,128)(2,1)S(1)}, u32[]{:S(2)}, u32[]{:S(2)}) %collective-permute-start.8) | collective-permute-done | bytes 524320 | tf_op jit(solution)/shard_map/ppermute | solution.py:353
  32.4 0.7 collective-permute-done.9.refs_7_
  33.1 14.8 %revalue.1 = (f32[128,8,128]{2,1,0:T(8,128)S(1)}, f32[128,8,128]{2,1,0:T(8,128)S(1)}, f32[128,128]{1,0:T(8,128)S(1)}, f32[16,2048]{1,0:T(8,128)}) custom-call(s32[32]{0:T(128)S(1)} %pad_add_fusion.slots, s32[8192]{0:T(1024)S(1)} %reshape.48.lists, s32[128]{0:T(128)S(1)} %copy-done, s32[128]{0:T(128)S(1)} %fusion.2.own, ...), custom_call_target="tpu_custom_call" | custom-call | tf_op jit(solution)/shard_map/revalue/pallas_call | solution.py:170
  47.9 0.2 collective-permute-start.10
  48.2 1.8 %collective-permute-done.10 = f32[128,8,128]{2,1,0:T(8,128)S(1)} collective-permute-done((f32[128,8,128]{2,1,0:T(8,128)S(1)}, f32[128,8,128]{2,1,0:T(8,128)S(1)}, u32[]{:S(2)}, u32[]{:S(2)}) %collective-permute-start.10) | collective-permute-done | bytes 524320 | tf_op jit(solution)/shard_map/ppermute | solution.py:371
  50.0 16.6 %all_to_all.10.p_ref = f32[16,64,128]{2,1,0:T(8,128)S(1)} all-to-all(f32[16,64,128]{2,1,0:T(8,128)S(1)} %bitcast.4), channel_id=1, replica_groups={{0,16,32,48,64,80,96,112,128,144,160,176,192,208,224,240},{8,24,40,56,7..., dimensions={0} | all-to-all | bytes 1048576 | tf_op jit(solution)/shard_map/all_to_all | solution.py:373
  66.6 0.3 moments.1
  66.9 16.6 %all_to_all.11.p_ref = f32[8,16,128]{2,1,0:T(8,128)S(1)} all-to-all(f32[8,16,128]{2,1,0:T(8,128)S(1)} %get-tuple-element.15), channel_id=1, replica_groups=mesh['set'=32,'path'=8] {'path'}, dimensions={0} | all-to-all | bytes 131072 | tf_op jit(solution)/shard_map/all_to_all | solution.py:377
  83.6 2.2 %expose.1 = f32[2,8,512]{2,1,0:T(8,128)} custom-call(f32[8,16,128]{2,1,0:T(8,128)S(1)} %all_to_all.11.p_ref, f32[64,128]{1,0:T(8,128)S(1)} %get-tuple-element.16.n_ref, f32[128,128]{1,0:T(8,128)S(1)} %get-tuple-element.14.b_ref), custom_call_target="tpu_custom_call" | custom-call | tf_op jit(solution)/shard_map/expose/pallas_call | solution.py:278
  (29 shorter events, 0.4 us)
Async XLA Ops:
  0.6 18.4 %copy-start.4 = (s32[4]{0:T(128)S(1)}, s32[4]{0:T(128)}, u32[]{:S(2)}) copy-start(s32[4]{0:T(128)} %constant.120.clone) | copy-start | bytes 52
  0.6 18.7 %copy-start.1 = (bf16[128,64,64]{0,2,1:T(8,128)(2,1)S(1)}, bf16[128,64,64]{0,2,1:T(8,128)(2,1)}, u32[]{:S(2)}) copy-start(bf16[128,64,64]{0,2,1:T(8,128)(2,1)} %param.16) | copy-start | bytes 3145732
  0.7 22.6 %copy-start.3 = (bf16[128,64]{0,1:T(8,128)(2,1)S(1)}, bf16[128,64]{0,1:T(8,128)(2,1)}, u32[]{:S(2)}) copy-start(bf16[128,64]{0,1:T(8,128)(2,1)} %param.15) | copy-start | bytes 49156
  0.7 23.3 %copy-start.2 = (s32[128,64]{0,1:T(8,128)S(1)}, s32[128,64]{0,1:T(8,128)}, u32[]{:S(2)}) copy-start(s32[128,64]{0,1:T(8,128)} %param.14) | copy-start | bytes 98308
  5.0 6.6 %collective-permute-start = (bf16[32,2048]{1,0:T(8,128)(2,1)S(1)}, bf16[32,2048]{1,0:T(8,128)(2,1)S(1)}, u32[]{:S(2)}, u32[]{:S(2)}) collective-permute-start(bf16[32,2048]{1,0:T(8,128)(2,1)S(1)} %get-tuple-element.10), channel_id=1, source_target_pairs={{0,32},{8,136},{16,48},{24,152},{32,0},{40,168},{48,16},{56,184},{... | collective-permute-start | bytes 393224 | tf_op jit(solution)/shard_map/ppermute | solution.py:350
  7.3 5.8 %collective-permute-start.1 = (bf16[32,2048]{1,0:T(8,128)(2,1)S(1)}, bf16[32,2048]{1,0:T(8,128)(2,1)S(1)}, u32[]{:S(2)}, u32[]{:S(2)}) collective-permute-start(bf16[32,2048]{1,0:T(8,128)(2,1)S(1)} %get-tuple-element.10), channel_id=1, source_target_pairs={{0,48},{8,200},{16,0},{24,216},{32,16},{40,232},{48,32},{56,248},{... | collective-permute-start | bytes 393224 | tf_op jit(solution)/shard_map/ppermute | solution.py:350
  8.7 5.0 %collective-permute-start.2 = (bf16[32,2048]{1,0:T(8,128)(2,1)S(1)}, bf16[32,2048]{1,0:T(8,128)(2,1)S(1)}, u32[]{:S(2)}, u32[]{:S(2)}) collective-permute-start(bf16[32,2048]{1,0:T(8,128)(2,1)S(1)} %get-tuple-element.10), channel_id=1, source_target_pairs={{0,16},{8,72},{16,32},{24,88},{32,48},{40,104},{48,0},{56,120},{64... | collective-permute-start | bytes 393224 | tf_op jit(solution)/shard_map/ppermute | solution.py:350
  13.7 14.4 %collective-permute-start.3 = (bf16[128,2048]{1,0:T(8,128)(2,1)S(1)}, bf16[128,2048]{1,0:T(8,128)(2,1)S(1)}, u32[]{:S(2)}, u32[]{:S(2)}) collective-permute-start(bf16[128,2048]{1,0:T(8,128)(2,1)S(1)} %constant_dynamic-update-slice_fusion.refs_0_), channel_id=1, source_target_pairs={{0,128},{8,40},{16,144},{24,56},{32,160},{40,8},{48,176},{56,24},{... | collective-permute-start | bytes 1572872 | tf_op jit(solution)/shard_map/ppermute | solution.py:352
  17.0 13.5 %collective-permute-start.4 = (bf16[128,2048]{1,0:T(8,128)(2,1)S(1)}, bf16[128,2048]{1,0:T(8,128)(2,1)S(1)}, u32[]{:S(2)}, u32[]{:S(2)}) collective-permute-start(bf16[128,2048]{1,0:T(8,128)(2,1)S(1)} %constant_dynamic-update-slice_fusion.refs_0_), channel_id=1, source_target_pairs={{0,192},{8,56},{16,208},{24,8},{32,224},{40,24},{48,240},{56,40},{... | collective-permute-start | bytes 1572872 | tf_op jit(solution)/shard_map/ppermute | solution.py:352
  18.0 12.4 %collective-permute-start.5 = (bf16[128,2048]{1,0:T(8,128)(2,1)S(1)}, bf16[128,2048]{1,0:T(8,128)(2,1)S(1)}, u32[]{:S(2)}, u32[]{:S(2)}) collective-permute-start(bf16[128,2048]{1,0:T(8,128)(2,1)S(1)} %constant_dynamic-update-slice_fusion.refs_0_), channel_id=1, source_target_pairs={{0,64},{8,24},{16,80},{24,40},{32,96},{40,56},{48,112},{56,8},{64,... | collective-permute-start | bytes 1572872 | tf_op jit(solution)/shard_map/ppermute | solution.py:352
  19.4 11.7 %copy-start.5 = (s32[128]{0:T(128)S(1)}, s32[128]{0:T(128)}, u32[]{:S(2)}) copy-start(s32[128]{0:T(128)} %param.18) | copy-start | bytes 1540
  19.4 13.7 %copy-start = (s32[128]{0:T(128)S(1)}, s32[128]{0:T(128)}, u32[]{:S(2)}) copy-start(s32[128]{0:T(128)} %cur.1) | copy-start | bytes 1540
  28.1 3.0 %collective-permute-start.6 = (bf16[128,2048]{1,0:T(8,128)(2,1)S(1)}, bf16[128,2048]{1,0:T(8,128)(2,1)S(1)}, u32[]{:S(2)}, u32[]{:S(2)}) collective-permute-start(bf16[128,2048]{1,0:T(8,128)(2,1)S(1)} %constant_dynamic-update-slice_fusion.refs_0_), channel_id=1, source_target_pairs={{0,8},{8,0},{16,24},{24,16},{32,40},{40,32},{48,56},{56,48},{64,72... | collective-permute-start | bytes 1572872 | tf_op jit(solution)/shard_map/ppermute | solution.py:353
  28.1 3.0 %collective-permute-start.7 = (bf16[128,2048]{1,0:T(8,128)(2,1)S(1)}, bf16[128,2048]{1,0:T(8,128)(2,1)S(1)}, u32[]{:S(2)}, u32[]{:S(2)}) collective-permute-start(bf16[128,2048]{1,0:T(8,128)(2,1)S(1)} %collective-permute-done.3.refs_1_), channel_id=1, source_target_pairs={{0,8},{8,0},{16,24},{24,16},{32,40},{40,32},{48,56},{56,48},{64,72... | collective-permute-start | bytes 1572872 | tf_op jit(solution)/shard_map/ppermute | solution.py:353
  30.4 1.9 %collective-permute-start.8 = (bf16[128,2048]{1,0:T(8,128)(2,1)S(1)}, bf16[128,2048]{1,0:T(8,128)(2,1)S(1)}, u32[]{:S(2)}, u32[]{:S(2)}) collective-permute-start(bf16[128,2048]{1,0:T(8,128)(2,1)S(1)} %collective-permute-done.4.refs_2_), channel_id=1, source_target_pairs={{0,8},{8,0},{16,24},{24,16},{32,40},{40,32},{48,56},{56,48},{64,72... | collective-permute-start | bytes 1572872 | tf_op jit(solution)/shard_map/ppermute | solution.py:353
  30.5 2.7 %collective-permute-start.9 = (bf16[128,2048]{1,0:T(8,128)(2,1)S(1)}, bf16[128,2048]{1,0:T(8,128)(2,1)S(1)}, u32[]{:S(2)}, u32[]{:S(2)}) collective-permute-start(bf16[128,2048]{1,0:T(8,128)(2,1)S(1)} %collective-permute-done.5.refs_3_), channel_id=1, source_target_pairs={{0,8},{8,0},{16,24},{24,16},{32,40},{40,32},{48,56},{56,48},{64,72... | collective-permute-start | bytes 1572872 | tf_op jit(solution)/shard_map/ppermute | solution.py:353
  47.9 2.0 %collective-permute-start.10 = (f32[128,8,128]{2,1,0:T(8,128)S(1)}, f32[128,8,128]{2,1,0:T(8,128)S(1)}, u32[]{:S(2)}, u32[]{:S(2)}) collective-permute-start(f32[128,8,128]{2,1,0:T(8,128)S(1)} %get-tuple-element.13), channel_id=1, source_target_pairs={{0,8},{8,0},{16,24},{24,16},{32,40},{40,32},{48,56},{56,48},{64,72... | collective-permute-start | bytes 1572872 | tf_op jit(solution)/shard_map/ppermute | solution.py:371

commit v5 on v4

--- a/solution.py
+++ b/solution.py
@@ -256,19 +256,32 @@
                 pltpu.roll(rest, LANES - 2 * NBP, 1),
             ], axis=0)
             sys.append(jnp.where(lane < NBP, a, 0.0) + diag)
+        at = lax.broadcasted_iota(jnp.int32, (NBP, LANES), 0)
+        col = lax.broadcasted_iota(jnp.int32, (NBP, LANES), 1)
+        rows = []
+        for t in range(STEPS):
+            turned = jnp.transpose(sys[t][NBP:])[:NBP]
+            rows.append(
+                [jnp.broadcast_to(sys[t][:NBP, i:i + 1], (NBP, LANES)) for i in range(NB + 1)]
+                + [jnp.broadcast_to(turned[:, c:c + 1], (NBP, LANES)) for c in range(SUB)]
+            )
         for k in range(NB + 1):
             for t in range(STEPS):
-                a = sys[t]
-                r = a[k:k + 1, :]
-                c = a[:, k:k + 1] * (1.0 / a[k:k + 1, k:k + 1])
-                sys[t] = jnp.where(lane == k, c, a - c * r)
+                v = rows[t]
+                inv = 1.0 / v[k][k:k + 1]
+                w = v[k] * inv
+                for i in range(k + 1, len(v)):
+                    mine = v[i][k:k + 1]
+                    v[i] = jnp.where(at == k, mine * inv, v[i] - mine * w)
         for t in range(STEPS):
-            coef = sys[t][NBP:, 0:NBP]
+            coef = jnp.zeros((NBP, LANES), F32)
+            for c in range(SUB):
+                coef = jnp.where(col == c, rows[t][NB + 1 + c], coef)
             steps = [t * chunks + q for q in range(chunks)]
-            fitted = jnp.dot(
-                coef, jnp.concatenate([basis_rows(b_ref, s) for s in steps], axis=1),
+            fitted = lax.dot_general(
+                coef, jnp.concatenate([basis_rows(b_ref, s) for s in steps], axis=1), (((0,), (0,)), ((), ())),
                 precision=HIGH, preferred_element_type=F32,
-            )
+            )[:SUB]
             n = jnp.concatenate([n_ref[pl.ds(s, SUB, stride=SUB), :] for s in steps], axis=1)
             o_ref[t] = jnp.maximum(n - 0.9 * fitted, 0.0)
         cp = pltpu.make_async_copy(o_ref, o_hbm, sem)

time: 86 us -> 85.9 us (level)
  no operation moved by 1% of the time
where the time goes in v5:
time: 85.9 us; the launch traced here: 85.7 us
  blocking collectives  33.2 us (39%)
  Pallas kernels  25.4 us (30%)
  starting transfers between devices  10.8 us (13%)
  waiting for transfers between devices  10 us (12%)
  local copies, waits for them, and re-layouts  5.32 us (6%)
    all_to_all x1, blocking collectives, per_device(): payload = lax.all_to_all(payload, 'path', 0, 0)  16.7 us
    all_to_all x1, blocking collectives, per_device(): lax.all_to_all(mine.reshape(GRID * GRID, SUB * SUB, LANES), 'set', 0, 0,...  16.5 us
    pallas_call x1, Pallas kernels, revalue(): pl.pallas_call(body, in_specs=[smem] * 4 + [vmem] * len(arrays) + [hbm, v...  14.8 us
    ppermute x3, starting transfers between devices, per_device(): lax.ppermute(line, 'set', hop_pairs(h, 1))  5.31 us
    unnamed x17, local copies, waits for them, and re-layouts  4.61 us
    pallas_call x1, Pallas kernels, evolve(): pl.pallas_call(body, in_specs=[hbm] * 4, out_specs=(vmem, vmem), out_shap...  4.36 us
    ppermute x3, waiting for transfers between devices, per_device(): lax.ppermute(slab, 'set', hop_pairs(h, 0))  4.34 us
    ppermute x3, starting transfers between devices, per_device(): lax.ppermute(slab, 'set', hop_pairs(h, 0))  4.24 us
  transfers between devices with their start and end apart: 11, of which 7 were waited for; matrix products, arithmetic and copies ran while one was open for 6% of the time, Pallas kernels for 4%

profile of v5, /device:TPU:2, one launch (start us, length us, event | category | flops | bytes accessed | tf_op | source)
XLA Modules:
  0.0 85.7 jit_solution(9218316119140367463)
XLA Ops:
  0.7 4.4 %evolve.1 = (bf16[32,2048]{1,0:T(8,128)(2,1)S(1)}, f32[16,2048]{1,0:T(8,128)S(1)}) custom-call(bf16[32,2048]{1,0:T(8,128)(2,1)} %bitcast.5, bf16[2048,2048]{1,0:T(8,128)(2,1)} %l_hbm.1, f32[16,2048]{1,0:T(8,128)} %s_hbm.1, f32[1,2048]{1,0:T(1,128)} %bitcast.7), custom_call_target="tpu_custom_call" | custom-call | tf_op jit(solution)/shard_map/evolve/pallas_call | solution.py:335
  5.0 2.2 %collective-permute-start = (bf16[32,2048]{1,0:T(8,128)(2,1)S(1)}, bf16[32,2048]{1,0:T(8,128)(2,1)S(1)}, u32[]{:S(2)}, u32[]{:S(2)}) collective-permute-start(bf16[32,2048]{1,0:T(8,128)(2,1)S(1)} %get-tuple-element.10), channel_id=1, source_target_pairs={{0,32},{8,136},{16,48},{24,152},{32,0},{40,168},{48,16},{56,184},{... | collective-permute-start | bytes 393224 | tf_op jit(solution)/shard_map/ppermute | solution.py:363
  7.3 1.4 %collective-permute-start.1 = (bf16[32,2048]{1,0:T(8,128)(2,1)S(1)}, bf16[32,2048]{1,0:T(8,128)(2,1)S(1)}, u32[]{:S(2)}, u32[]{:S(2)}) collective-permute-start(bf16[32,2048]{1,0:T(8,128)(2,1)S(1)} %get-tuple-element.10), channel_id=1, source_target_pairs={{0,48},{8,200},{16,0},{24,216},{32,16},{40,232},{48,32},{56,248},{... | collective-permute-start | bytes 393224 | tf_op jit(solution)/shard_map/ppermute | solution.py:363
  8.7 0.6 collective-permute-start.2
  9.3 2.4 %collective-permute-done = bf16[32,2048]{1,0:T(8,128)(2,1)S(1)} collective-permute-done((bf16[32,2048]{1,0:T(8,128)(2,1)S(1)}, bf16[32,2048]{1,0:T(8,128)(2,1)S(1)}, u32[]{:S(2)}, u32[]{:S(2)}) %collective-permute-start) | collective-permute-done | bytes 131104 | tf_op jit(solution)/shard_map/ppermute | solution.py:363
  11.7 1.3 %collective-permute-done.1 = bf16[32,2048]{1,0:T(8,128)(2,1)S(1)} collective-permute-done((bf16[32,2048]{1,0:T(8,128)(2,1)S(1)}, bf16[32,2048]{1,0:T(8,128)(2,1)S(1)}, u32[]{:S(2)}, u32[]{:S(2)}) %collective-permute-start.1) | collective-permute-done | bytes 131104 | tf_op jit(solution)/shard_map/ppermute | solution.py:363
  13.0 0.6 collective-permute-done.2
  13.7 3.3 %collective-permute-start.3 = (bf16[128,2048]{1,0:T(8,128)(2,1)S(1)}, bf16[128,2048]{1,0:T(8,128)(2,1)S(1)}, u32[]{:S(2)}, u32[]{:S(2)}) collective-permute-start(bf16[128,2048]{1,0:T(8,128)(2,1)S(1)} %constant_dynamic-update-slice_fusion.refs_0_), channel_id=1, source_target_pairs={{0,128},{8,40},{16,144},{24,56},{32,160},{40,8},{48,176},{56,24},{... | collective-permute-start | bytes 1572872 | tf_op jit(solution)/shard_map/ppermute | solution.py:365
  17.0 1.1 %collective-permute-start.4 = (bf16[128,2048]{1,0:T(8,128)(2,1)S(1)}, bf16[128,2048]{1,0:T(8,128)(2,1)S(1)}, u32[]{:S(2)}, u32[]{:S(2)}) collective-permute-start(bf16[128,2048]{1,0:T(8,128)(2,1)S(1)} %constant_dynamic-update-slice_fusion.refs_0_), channel_id=1, source_target_pairs={{0,192},{8,56},{16,208},{24,8},{32,224},{40,24},{48,240},{56,40},{... | collective-permute-start | bytes 1572872 | tf_op jit(solution)/shard_map/ppermute | solution.py:365
  18.0 1.0 %collective-permute-start.5 = (bf16[128,2048]{1,0:T(8,128)(2,1)S(1)}, bf16[128,2048]{1,0:T(8,128)(2,1)S(1)}, u32[]{:S(2)}, u32[]{:S(2)}) collective-permute-start(bf16[128,2048]{1,0:T(8,128)(2,1)S(1)} %constant_dynamic-update-slice_fusion.refs_0_), channel_id=1, source_target_pairs={{0,64},{8,24},{16,80},{24,40},{32,96},{40,56},{48,112},{56,8},{64,... | collective-permute-start | bytes 1572872 | tf_op jit(solution)/shard_map/ppermute | solution.py:365
  19.1 0.1 sub.59
  19.1 0.1 sub.63
  19.3 0.1 sub.68
  19.4 3.8 %copy.16.g_ref = bf16[128,64,64]{2,1,0:T(8,128)(2,1)} copy(bf16[128,64,64]{0,2,1:T(8,128)(2,1)S(1)} %copy-done.1) | data formatting | bytes 2097152 | tf_op args[6]
  23.2 0.7 copy.17.d_ref
  24.0 0.1 copy.14
  24.1 0.1 reshape.47
  24.1 0.1 copy.15
  24.2 0.1 reshape.48.lists
  24.4 3.7 %prepare.1.refs_8_ = bf16[32,272,256]{2,1,0:T(8,128)(2,1)} custom-call(bf16[128,64,64]{2,1,0:T(8,128)(2,1)} %copy.16.g_ref, bf16[128,64]{1,0:T(8,128)(2,1)} %copy.17.d_ref), custom_call_target="tpu_custom_call" | custom-call | tf_op jit(solution)/shard_map/prepare/pallas_call | solution.py:68
  28.1 0.5 collective-permute-start.7
  28.6 1.9 %collective-permute-done.4.refs_2_ = bf16[128,2048]{1,0:T(8,128)(2,1)S(1)} collective-permute-done((bf16[128,2048]{1,0:T(8,128)(2,1)S(1)}, bf16[128,2048]{1,0:T(8,128)(2,1)S(1)}, u32[]{:S(2)}, u32[]{:S(2)}) %collective-permute-start.4) | collective-permute-done | bytes 524320 | tf_op jit(solution)/shard_map/ppermute | solution.py:365
  30.5 0.5 collective-permute-start.9
  31.1 1.3 %collective-permute-done.8.refs_6_ = bf16[128,2048]{1,0:T(8,128)(2,1)S(1)} collective-permute-done((bf16[128,2048]{1,0:T(8,128)(2,1)S(1)}, bf16[128,2048]{1,0:T(8,128)(2,1)S(1)}, u32[]{:S(2)}, u32[]{:S(2)}) %collective-permute-start.8) | collective-permute-done | bytes 524320 | tf_op jit(solution)/shard_map/ppermute | solution.py:366
  32.4 0.7 collective-permute-done.9.refs_7_
  33.1 14.8 %revalue.1 = (f32[128,8,128]{2,1,0:T(8,128)S(1)}, f32[128,8,128]{2,1,0:T(8,128)S(1)}, f32[128,128]{1,0:T(8,128)S(1)}, f32[16,2048]{1,0:T(8,128)}) custom-call(s32[32]{0:T(128)S(1)} %pad_add_fusion.slots, s32[8192]{0:T(1024)S(1)} %reshape.48.lists, s32[128]{0:T(128)S(1)} %copy-done, s32[128]{0:T(128)S(1)} %fusion.2.own, ...), custom_call_target="tpu_custom_call" | custom-call | tf_op jit(solution)/shard_map/revalue/pallas_call | solution.py:170
  48.0 0.2 collective-permute-start.10
  48.2 1.8 %collective-permute-done.10 = f32[128,8,128]{2,1,0:T(8,128)S(1)} collective-permute-done((f32[128,8,128]{2,1,0:T(8,128)S(1)}, f32[128,8,128]{2,1,0:T(8,128)S(1)}, u32[]{:S(2)}, u32[]{:S(2)}) %collective-permute-start.10) | collective-permute-done | bytes 524320 | tf_op jit(solution)/shard_map/ppermute | solution.py:384
  50.0 16.5 %all_to_all.10.p_ref = f32[16,64,128]{2,1,0:T(8,128)S(1)} all-to-all(f32[16,64,128]{2,1,0:T(8,128)S(1)} %bitcast.4), channel_id=1, replica_groups={{0,16,32,48,64,80,96,112,128,144,160,176,192,208,224,240},{8,24,40,56,7..., dimensions={0} | all-to-all | bytes 1048576 | tf_op jit(solution)/shard_map/all_to_all | solution.py:386
  66.6 0.3 moments.1
  66.9 16.7 %all_to_all.11.p_ref = f32[8,16,128]{2,1,0:T(8,128)S(1)} all-to-all(f32[8,16,128]{2,1,0:T(8,128)S(1)} %get-tuple-element.15), channel_id=1, replica_groups=mesh['set'=32,'path'=8] {'path'}, dimensions={0} | all-to-all | bytes 131072 | tf_op jit(solution)/shard_map/all_to_all | solution.py:390
  83.6 2.1 %expose.1 = f32[2,8,512]{2,1,0:T(8,128)} custom-call(f32[8,16,128]{2,1,0:T(8,128)S(1)} %all_to_all.11.p_ref, f32[64,128]{1,0:T(8,128)S(1)} %get-tuple-element.16.n_ref, f32[128,128]{1,0:T(8,128)S(1)} %get-tuple-element.14.b_ref), custom_call_target="tpu_custom_call" | custom-call | tf_op jit(solution)/shard_map/expose/pallas_call | solution.py:291
  (29 shorter events, 0.4 us)
Async XLA Ops:
  0.6 18.4 %copy-start.4 = (s32[4]{0:T(128)S(1)}, s32[4]{0:T(128)}, u32[]{:S(2)}) copy-start(s32[4]{0:T(128)} %constant.120.clone) | copy-start | bytes 52
  0.6 18.7 %copy-start.1 = (bf16[128,64,64]{0,2,1:T(8,128)(2,1)S(1)}, bf16[128,64,64]{0,2,1:T(8,128)(2,1)}, u32[]{:S(2)}) copy-start(bf16[128,64,64]{0,2,1:T(8,128)(2,1)} %param.16) | copy-start | bytes 3145732
  0.7 22.6 %copy-start.3 = (bf16[128,64]{0,1:T(8,128)(2,1)S(1)}, bf16[128,64]{0,1:T(8,128)(2,1)}, u32[]{:S(2)}) copy-start(bf16[128,64]{0,1:T(8,128)(2,1)} %param.15) | copy-start | bytes 49156
  0.7 23.3 %copy-start.2 = (s32[128,64]{0,1:T(8,128)S(1)}, s32[128,64]{0,1:T(8,128)}, u32[]{:S(2)}) copy-start(s32[128,64]{0,1:T(8,128)} %param.14) | copy-start | bytes 98308
  5.0 6.6 %collective-permute-start = (bf16[32,2048]{1,0:T(8,128)(2,1)S(1)}, bf16[32,2048]{1,0:T(8,128)(2,1)S(1)}, u32[]{:S(2)}, u32[]{:S(2)}) collective-permute-start(bf16[32,2048]{1,0:T(8,128)(2,1)S(1)} %get-tuple-element.10), channel_id=1, source_target_pairs={{0,32},{8,136},{16,48},{24,152},{32,0},{40,168},{48,16},{56,184},{... | collective-permute-start | bytes 393224 | tf_op jit(solution)/shard_map/ppermute | solution.py:363
  7.3 5.8 %collective-permute-start.1 = (bf16[32,2048]{1,0:T(8,128)(2,1)S(1)}, bf16[32,2048]{1,0:T(8,128)(2,1)S(1)}, u32[]{:S(2)}, u32[]{:S(2)}) collective-permute-start(bf16[32,2048]{1,0:T(8,128)(2,1)S(1)} %get-tuple-element.10), channel_id=1, source_target_pairs={{0,48},{8,200},{16,0},{24,216},{32,16},{40,232},{48,32},{56,248},{... | collective-permute-start | bytes 393224 | tf_op jit(solution)/shard_map/ppermute | solution.py:363
  8.7 5.0 %collective-permute-start.2 = (bf16[32,2048]{1,0:T(8,128)(2,1)S(1)}, bf16[32,2048]{1,0:T(8,128)(2,1)S(1)}, u32[]{:S(2)}, u32[]{:S(2)}) collective-permute-start(bf16[32,2048]{1,0:T(8,128)(2,1)S(1)} %get-tuple-element.10), channel_id=1, source_target_pairs={{0,16},{8,72},{16,32},{24,88},{32,48},{40,104},{48,0},{56,120},{64... | collective-permute-start | bytes 393224 | tf_op jit(solution)/shard_map/ppermute | solution.py:363
  13.7 14.4 %collective-permute-start.3 = (bf16[128,2048]{1,0:T(8,128)(2,1)S(1)}, bf16[128,2048]{1,0:T(8,128)(2,1)S(1)}, u32[]{:S(2)}, u32[]{:S(2)}) collective-permute-start(bf16[128,2048]{1,0:T(8,128)(2,1)S(1)} %constant_dynamic-update-slice_fusion.refs_0_), channel_id=1, source_target_pairs={{0,128},{8,40},{16,144},{24,56},{32,160},{40,8},{48,176},{56,24},{... | collective-permute-start | bytes 1572872 | tf_op jit(solution)/shard_map/ppermute | solution.py:365
  17.0 13.5 %collective-permute-start.4 = (bf16[128,2048]{1,0:T(8,128)(2,1)S(1)}, bf16[128,2048]{1,0:T(8,128)(2,1)S(1)}, u32[]{:S(2)}, u32[]{:S(2)}) collective-permute-start(bf16[128,2048]{1,0:T(8,128)(2,1)S(1)} %constant_dynamic-update-slice_fusion.refs_0_), channel_id=1, source_target_pairs={{0,192},{8,56},{16,208},{24,8},{32,224},{40,24},{48,240},{56,40},{... | collective-permute-start | bytes 1572872 | tf_op jit(solution)/shard_map/ppermute | solution.py:365
  18.0 12.4 %collective-permute-start.5 = (bf16[128,2048]{1,0:T(8,128)(2,1)S(1)}, bf16[128,2048]{1,0:T(8,128)(2,1)S(1)}, u32[]{:S(2)}, u32[]{:S(2)}) collective-permute-start(bf16[128,2048]{1,0:T(8,128)(2,1)S(1)} %constant_dynamic-update-slice_fusion.refs_0_), channel_id=1, source_target_pairs={{0,64},{8,24},{16,80},{24,40},{32,96},{40,56},{48,112},{56,8},{64,... | collective-permute-start | bytes 1572872 | tf_op jit(solution)/shard_map/ppermute | solution.py:365
  19.4 11.7 %copy-start.5 = (s32[128]{0:T(128)S(1)}, s32[128]{0:T(128)}, u32[]{:S(2)}) copy-start(s32[128]{0:T(128)} %param.18) | copy-start | bytes 1540
  19.4 13.7 %copy-start = (s32[128]{0:T(128)S(1)}, s32[128]{0:T(128)}, u32[]{:S(2)}) copy-start(s32[128]{0:T(128)} %cur.1) | copy-start | bytes 1540
  28.1 3.0 %collective-permute-start.6 = (bf16[128,2048]{1,0:T(8,128)(2,1)S(1)}, bf16[128,2048]{1,0:T(8,128)(2,1)S(1)}, u32[]{:S(2)}, u32[]{:S(2)}) collective-permute-start(bf16[128,2048]{1,0:T(8,128)(2,1)S(1)} %constant_dynamic-update-slice_fusion.refs_0_), channel_id=1, source_target_pairs={{0,8},{8,0},{16,24},{24,16},{32,40},{40,32},{48,56},{56,48},{64,72... | collective-permute-start | bytes 1572872 | tf_op jit(solution)/shard_map/ppermute | solution.py:366
  28.1 3.0 %collective-permute-start.7 = (bf16[128,2048]{1,0:T(8,128)(2,1)S(1)}, bf16[128,2048]{1,0:T(8,128)(2,1)S(1)}, u32[]{:S(2)}, u32[]{:S(2)}) collective-permute-start(bf16[128,2048]{1,0:T(8,128)(2,1)S(1)} %collective-permute-done.3.refs_1_), channel_id=1, source_target_pairs={{0,8},{8,0},{16,24},{24,16},{32,40},{40,32},{48,56},{56,48},{64,72... | collective-permute-start | bytes 1572872 | tf_op jit(solution)/shard_map/ppermute | solution.py:366
  30.4 1.9 %collective-permute-start.8 = (bf16[128,2048]{1,0:T(8,128)(2,1)S(1)}, bf16[128,2048]{1,0:T(8,128)(2,1)S(1)}, u32[]{:S(2)}, u32[]{:S(2)}) collective-permute-start(bf16[128,2048]{1,0:T(8,128)(2,1)S(1)} %collective-permute-done.4.refs_2_), channel_id=1, source_target_pairs={{0,8},{8,0},{16,24},{24,16},{32,40},{40,32},{48,56},{56,48},{64,72... | collective-permute-start | bytes 1572872 | tf_op jit(solution)/shard_map/ppermute | solution.py:366
  30.5 2.7 %collective-permute-start.9 = (bf16[128,2048]{1,0:T(8,128)(2,1)S(1)}, bf16[128,2048]{1,0:T(8,128)(2,1)S(1)}, u32[]{:S(2)}, u32[]{:S(2)}) collective-permute-start(bf16[128,2048]{1,0:T(8,128)(2,1)S(1)} %collective-permute-done.5.refs_3_), channel_id=1, source_target_pairs={{0,8},{8,0},{16,24},{24,16},{32,40},{40,32},{48,56},{56,48},{64,72... | collective-permute-start | bytes 1572872 | tf_op jit(solution)/shard_map/ppermute | solution.py:366
  48.0 2.0 %collective-permute-start.10 = (f32[128,8,128]{2,1,0:T(8,128)S(1)}, f32[128,8,128]{2,1,0:T(8,128)S(1)}, u32[]{:S(2)}, u32[]{:S(2)}) collective-permute-start(f32[128,8,128]{2,1,0:T(8,128)S(1)} %get-tuple-element.13), channel_id=1, source_target_pairs={{0,8},{8,0},{16,24},{24,16},{32,40},{40,32},{48,56},{56,48},{64,72... | collective-permute-start | bytes 1572872 | tf_op jit(solution)/shard_map/ppermute | solution.py:384
